TPU v7x, 512 devices: a whole 4x4x16 slice. The times are simulated.
512 devices in a mesh: section: 16 (over y, x_hi, core), expert: 32 (over x_lo, z).
Axes of the slice: x: 4 (x_hi: 2, x_lo: 2; x = x_hi * 2 + x_lo), y: 4, z: 16, core: 2. Of those that a mesh axis runs over, the one named last changes fastest.
Arguments:
- act_in: bfloat16 [16, 4096, 2048], P('section', 'expert'), may hold values from -6 to 6
- saved_in: bfloat16 [16, 4096, 2048], P('section', 'expert'), may hold values from -6 to 6
- grad_in: bfloat16 [16, 4096, 2048], P('section', 'expert'), may hold values from -6 to 6
- norm_gain: float32 [16, 2048], P('section'), may hold values from 0.1 to 1.9
- w_gate: bfloat16 [16, 2048, 6144], P('section', None, 'expert'), may hold values from -0.125 to 0.125
- w_up: bfloat16 [16, 2048, 6144], P('section', None, 'expert'), may hold values from -0.125 to 0.125
- w_down: bfloat16 [16, 6144, 2048], P('section', 'expert'), may hold values from -0.21875 to 0.21875
- routes_fwd: int32 [16, 4096, 1], P('section', 'expert'), may hold values from 0 to 7; in each aligned block of 128 rows (0 to 127, 128 to 255, ..., all dimensions but the last counted through in order) at most 18 rows name the same one
- gates_fwd: float32 [16, 4096, 1], P('section', 'expert'), may hold values from 0.1 to 1
- routes_bwd: int32 [16, 4096, 1], P('section', 'expert'), may hold values from 0 to 7; in each aligned block of 128 rows (0 to 127, 128 to 255, ..., all dimensions but the last counted through in order) at most 18 rows name the same one
- gates_bwd: float32 [16, 4096, 1], P('section', 'expert'), may hold values from 0.1 to 1
Outputs:
- act_out: bfloat16 [16, 4096, 2048], P('section', 'expert')
- grad_out: bfloat16 [16, 4096, 2048], P('section', 'expert')
Inputs may be any that keep to these rules, and one draw needn't show every extreme that they name: `routes_fwd`: the 1 expert of a token differ; within the 128 tokens of one device no expert is named by more than 18 routes, and in some such blocks one expert is named by exactly 18. `routes_bwd`: as for routes_fwd.
All inputs are finite; a program needn't handle non-finite values.
Results may differ from a plain program's by a relative error of at most 0.005.
Values may be sent and summed in bfloat16 or wider, within the bound.
A program may use at most 64 MiB of HBM per device.

v0:
```python
import jax
import jax.numpy as jnp
from jax import lax
from jax.sharding import PartitionSpec as P

SPLIT = 4


norm_eps = 1e-06


def passed_along(value, axis, steps):
    count = lax.axis_size(axis)
    pairs = [(source, (source + steps) % count) for source in range(count)]
    return lax.ppermute(value, axis, pairs)


def silu_parts(values):
    sigma = jax.nn.sigmoid(values)
    return (values * sigma, sigma * (1.0 + values * (1.0 - sigma)))


def normalize(block_rows, gain_row):
    values = block_rows.astype(jnp.float32)
    inv_scale = lax.rsqrt(jnp.mean(values * values, axis=-1, keepdims=True) + norm_eps)
    return (values * inv_scale * gain_row, inv_scale)


def slot_chooser(routes, experts, capacity):
    tok_count, top_count = routes.shape
    flat_routes = routes.reshape(tok_count * top_count)
    onehot = (flat_routes[:, None] == jnp.arange(experts, dtype=jnp.int32)[None, :]).astype(
        jnp.int32
    )
    before = jnp.cumsum(onehot, axis=0) - onehot
    slot_index = jnp.sum(before * onehot, axis=1)
    target = flat_routes * capacity + slot_index
    picks = (jnp.arange(experts * capacity, dtype=jnp.int32)[:, None] == target[None, :]).astype(
        jnp.int32
    )
    chooser = jnp.sum(picks.reshape(experts * capacity, tok_count, top_count), axis=2).astype(
        jnp.bfloat16
    )
    return (chooser, target)


def fan_out(packed, experts, capacity):
    row_width = packed.shape[1]
    spread = jnp.broadcast_to(
        packed.reshape(experts, 1, capacity, row_width), (experts, SPLIT, capacity, row_width)
    )
    return spread.reshape(experts * SPLIT, capacity, row_width)


def combine(returned, target, gate_rows, experts):
    row_groups, capacity, row_width = returned.shape
    summed = jnp.sum(
        returned.reshape(experts, SPLIT, capacity, row_width).astype(jnp.float32), axis=1
    )
    picked = jnp.take(summed.reshape(experts * capacity, row_width), target, axis=0)
    tok_count, top_count = gate_rows.shape
    return jnp.sum(picked.reshape(tok_count, top_count, row_width) * gate_rows[:, :, None], axis=1)


def forward_rows(slot_rows, gate_w, up_w, down_w):
    row_groups, row_count, row_width = slot_rows.shape
    flat_rows = slot_rows.reshape(row_groups * row_count, row_width)
    gate_pre = jnp.dot(flat_rows, gate_w, preferred_element_type=jnp.float32)
    up_pre = jnp.dot(flat_rows, up_w, preferred_element_type=jnp.float32)
    activation, _ = silu_parts(gate_pre)
    hidden = (activation * up_pre).astype(jnp.bfloat16)
    partial_value = jnp.dot(hidden, down_w, preferred_element_type=jnp.float32).astype(jnp.bfloat16)
    return partial_value.reshape(row_groups, row_count, row_width)


def backward_rows(slot_rows, grad_rows, gate_w, up_w, down_w):
    row_groups, row_count, row_width = slot_rows.shape
    flat_rows = slot_rows.reshape(row_groups * row_count, row_width)
    flat_grads = grad_rows.reshape(row_groups * row_count, row_width)
    contract = (((1,), (1,)), ((), ()))
    gate_pre = jnp.dot(flat_rows, gate_w, preferred_element_type=jnp.float32)
    up_pre = jnp.dot(flat_rows, up_w, preferred_element_type=jnp.float32)
    activation, derivative = silu_parts(gate_pre)
    d_hidden = lax.dot_general(flat_grads, down_w, contract, preferred_element_type=jnp.float32)
    d_gate = (d_hidden * up_pre * derivative).astype(jnp.bfloat16)
    d_up = (d_hidden * activation).astype(jnp.bfloat16)
    partial_value = lax.dot_general(d_gate, gate_w, contract, preferred_element_type=jnp.float32)
    partial_value = partial_value + lax.dot_general(
        d_up, up_w, contract, preferred_element_type=jnp.float32
    )
    return partial_value.astype(jnp.bfloat16).reshape(row_groups, row_count, row_width)


def per_device(
    act_in,
    saved_in,
    grad_in,
    norm_gain,
    w_gate,
    w_up,
    w_down,
    routes_fwd,
    gates_fwd,
    routes_bwd,
    gates_bwd,
):
    groups = lax.axis_size("expert")
    experts = groups // SPLIT
    tok_count = act_in.shape[1]
    top_count = routes_fwd.shape[2]
    capacity = min(tok_count, tok_count * top_count // experts + 2)
    gain_row = norm_gain[0]
    gate_w = w_gate[0]
    up_w = w_up[0]
    down_w = w_down[0]
    incoming = passed_along(act_in, "section", 1)[0]
    upstream = passed_along(grad_in, "section", -1)[0]
    n_fwd = normalize(incoming, gain_row)[0].astype(jnp.bfloat16)
    values_b, inv_scale = normalize(saved_in[0], gain_row)
    n_bwd = values_b.astype(jnp.bfloat16)
    chooser_f, target_f = slot_chooser(routes_fwd[0], experts, capacity)
    chooser_b, target_b = slot_chooser(routes_bwd[0], experts, capacity)
    packed_f = jnp.dot(chooser_f, n_fwd, preferred_element_type=jnp.float32).astype(jnp.bfloat16)
    packed_bg = jnp.dot(
        chooser_b, jnp.concatenate([n_bwd, upstream], axis=1), preferred_element_type=jnp.float32
    ).astype(jnp.bfloat16)
    width = n_fwd.shape[1]
    send_f = fan_out(packed_f, experts, capacity)
    send_b = fan_out(packed_bg[:, :width], experts, capacity)
    send_g = fan_out(packed_bg[:, width:], experts, capacity)
    back_f = lax.all_to_all(
        forward_rows(
            lax.all_to_all(send_f, "expert", split_axis=0, concat_axis=0, tiled=True),
            gate_w,
            up_w,
            down_w,
        ),
        "expert",
        split_axis=0,
        concat_axis=0,
        tiled=True,
    )
    back_b = lax.all_to_all(
        backward_rows(
            lax.all_to_all(send_b, "expert", split_axis=0, concat_axis=0, tiled=True),
            lax.all_to_all(send_g, "expert", split_axis=0, concat_axis=0, tiled=True),
            gate_w,
            up_w,
            down_w,
        ),
        "expert",
        split_axis=0,
        concat_axis=0,
        tiled=True,
    )
    mixed = combine(back_f, target_f, gates_fwd[0], experts)
    act_out = (incoming.astype(jnp.float32) + mixed).astype(jnp.bfloat16)
    d_norm = combine(back_b, target_b, gates_bwd[0], experts)
    scaled = d_norm * gain_row
    base = saved_in[0].astype(jnp.float32)
    d_input = inv_scale * (
        scaled - base * inv_scale * inv_scale * jnp.mean(scaled * base, axis=-1, keepdims=True)
    )
    grad_out = (upstream.astype(jnp.float32) + d_input).astype(jnp.bfloat16)
    return (act_out[None], grad_out[None])


def solution(mesh):
    in_specs = (
        P("section", "expert", None),
        P("section", "expert", None),
        P("section", "expert", None),
        P("section", None),
        P("section", None, "expert"),
        P("section", None, "expert"),
        P("section", "expert", None),
        P("section", "expert", None),
        P("section", "expert", None),
        P("section", "expert", None),
        P("section", "expert", None),
    )
    out_specs = (P("section", "expert", None), P("section", "expert", None))
    return jax.shard_map(
        per_device, mesh=mesh, in_specs=in_specs, out_specs=out_specs, check_vma=False
    )
```

profile of v0, /device:TPU:7, one launch (start us, length us, event | category | flops | bytes accessed | tf_op | source)
XLA Modules:
  0.0 784.0 jit_solution(11789557118686046455)
XLA Ops:
  0.6 4.7 collective-permute-start
  5.4 0.7 fusion.55
  6.3 0.8 select_reduce_fusion.1
  7.1 1.3 compare_and_fusion.1
  8.4 3.4 collective-permute-done
  11.8 0.2 fusion.17
  12.0 1.1 convolution_convert_fusion.2
  13.1 0.2 broadcast_in_dim.18
  13.3 2.1 broadcast_in_dim.19
  15.4 16.3 %all-to-all-start = ((bf16[32,18,2048]{2,1,0:T(8,128)(2,1)}), bf16[32,18,2048]{2,1,0:T(8,128)(2,1)}, u32[]{:S(2)}, u32[]{:S(2)}) async-start(bf16[32,18,2048]{2,1,0:T(8,128)(2,1)} %bitcast.68), calls=%async_computation | async-start | bytes 6291456 | tf_op jit(solution)/shard_map/all_to_all | solution.py:133
  31.7 4.3 collective-permute-start.1
  36.5 0.2 fusion.7
  36.7 0.5 compare_and_fusion
  37.3 0.2 fusion.9
  37.5 8.5 %collective-permute-done.1 = bf16[1,128,2048]{2,1,0:T(8,128)(2,1)S(1)} collective-permute-done((bf16[1,128,2048]{2,1,0:T(8,128)(2,1)S(1)}, bf16[1,128,2048]{2,1,0:T(8,128)(2,1)S(1)}, u32[]{:S(2)}, u32[]{:S(2)}) %collective-permute-start.1) | collective-permute-done | bytes 524320 | tf_op jit(solution)/shard_map/ppermute | solution.py:15
  45.9 0.8 copy-done.7
  46.7 0.5 convolution_convert_fusion
  47.5 120.9 %all-to-all-done = bf16[32,18,2048]{2,1,0:T(8,128)(2,1)} async-done(((bf16[32,18,2048]{2,1,0:T(8,128)(2,1)}), bf16[32,18,2048]{2,1,0:T(8,128)(2,1)}, u32[]{:S(2)}, u32[]{:S(2)}) %all-to-all-start) | async-done | bytes 2359328 | tf_op jit(solution)/shard_map/all_to_all | solution.py:133
  168.4 2.1 broadcast_in_dim.24
  170.5 12.3 %all-to-all-start.2 = ((bf16[32,18,2048]{2,1,0:T(8,128)(2,1)}), bf16[32,18,2048]{2,1,0:T(8,128)(2,1)}, u32[]{:S(2)}, u32[]{:S(2)}) async-start(bf16[32,18,2048]{2,1,0:T(8,128)(2,1)} %bitcast.70), calls=%async_computation.2 | async-start | bytes 6291456 | tf_op jit(solution)/shard_map/all_to_all | solution.py:146
  183.0 136.8 %all-to-all-done.2 = bf16[32,18,2048]{2,1,0:T(8,128)(2,1)} async-done(((bf16[32,18,2048]{2,1,0:T(8,128)(2,1)}), bf16[32,18,2048]{2,1,0:T(8,128)(2,1)}, u32[]{:S(2)}, u32[]{:S(2)}) %all-to-all-start.2) | async-done | bytes 2359328 | tf_op jit(solution)/shard_map/all_to_all | solution.py:146
  319.8 2.1 broadcast_in_dim.46
  321.8 12.0 %all-to-all-start.3 = ((bf16[32,18,2048]{2,1,0:T(8,128)(2,1)}), bf16[32,18,2048]{2,1,0:T(8,128)(2,1)}, u32[]{:S(2)}, u32[]{:S(2)}) async-start(bf16[32,18,2048]{2,1,0:T(8,128)(2,1)} %bitcast.69), calls=%async_computation.3 | async-start | bytes 6291456 | tf_op jit(solution)/shard_map/all_to_all | solution.py:145
  333.8 2.9 reshape.191
  336.8 2.9 fusion.36
  339.7 4.7 convolution_convert_fusion.1
  344.5 4.3 reshape.192
  348.7 122.1 %all-to-all-done.3 = bf16[32,18,2048]{2,1,0:T(8,128)(2,1)} async-done(((bf16[32,18,2048]{2,1,0:T(8,128)(2,1)}), bf16[32,18,2048]{2,1,0:T(8,128)(2,1)}, u32[]{:S(2)}, u32[]{:S(2)}) %all-to-all-start.3) | async-done | bytes 2359328 | tf_op jit(solution)/shard_map/all_to_all | solution.py:145
  470.8 11.9 %all-to-all-start.1 = ((bf16[32,18,2048]{2,1,0:T(8,128)(2,1)}), bf16[32,18,2048]{2,1,0:T(8,128)(2,1)}, u32[]{:S(2)}, u32[]{:S(2)}) async-start(bf16[32,18,2048]{2,1,0:T(8,128)(2,1)} %reshape.192), calls=%async_computation.1 | async-start | bytes 6291456 | tf_op jit(solution)/shard_map/all_to_all | solution.py:131
  482.8 4.4 reshape.195
  487.2 2.9 reshape.197
  490.1 3.7 fusion.25
  493.9 1.8 fusion.34
  495.6 5.7 fusion.6
  501.4 3.5 add_convert_fusion
  504.9 2.5 reshape.198
  507.4 112.3 %all-to-all-done.1 = bf16[32,18,2048]{2,1,0:T(8,128)(2,1)} async-done(((bf16[32,18,2048]{2,1,0:T(8,128)(2,1)}), bf16[32,18,2048]{2,1,0:T(8,128)(2,1)}, u32[]{:S(2)}, u32[]{:S(2)}) %all-to-all-start.1) | async-done | bytes 2359328 | tf_op jit(solution)/shard_map/all_to_all | solution.py:131
  619.6 12.1 %all-to-all-start.4 = ((bf16[32,18,2048]{2,1,0:T(8,128)(2,1)}), bf16[32,18,2048]{2,1,0:T(8,128)(2,1)}, u32[]{:S(2)}, u32[]{:S(2)}) async-start(bf16[32,18,2048]{2,1,0:T(8,128)(2,1)} %reshape.198), calls=%async_computation.4 | async-start | bytes 6291456 | tf_op jit(solution)/shard_map/all_to_all | solution.py:143
  631.8 2.6 convert_reduce_fusion.1
  634.6 134.2 %all-to-all-done.4 = bf16[32,18,2048]{2,1,0:T(8,128)(2,1)} async-done(((bf16[32,18,2048]{2,1,0:T(8,128)(2,1)}), bf16[32,18,2048]{2,1,0:T(8,128)(2,1)}, u32[]{:S(2)}, u32[]{:S(2)}) %all-to-all-start.4) | async-done | bytes 2359328 | tf_op jit(solution)/shard_map/all_to_all | solution.py:143
  768.8 3.8 convert_reduce_fusion
  772.6 1.6 reshape.199
  774.2 2.0 gather_fusion.1
  776.1 1.7 fusion.10
  777.9 0.6 broadcast_multiply_fusion
  778.4 1.9 gather_fusion
  780.4 2.5 fusion.16
  782.9 1.1 fusion.20
  (49 shorter events, 1.3 us)
Async XLA Ops:
  0.6 339.1 %copy-start = (bf16[1,2048,192]{1,2,0:T(8,128)(2,1)S(1)}, bf16[1,2048,192]{1,2,0:T(8,128)(2,1)}, u32[]{:S(2)}) copy-start(bf16[1,2048,192]{1,2,0:T(8,128)(2,1)} %param.18) | copy-start | bytes 2359300
  0.6 11.2 %collective-permute-start = (bf16[1,128,2048]{2,1,0:T(8,128)(2,1)}, bf16[1,128,2048]{2,1,0:T(8,128)(2,1)S(1)}, u32[]{:S(2)}, u32[]{:S(2)}) collective-permute-start(bf16[1,128,2048]{2,1,0:T(8,128)(2,1)} %param.13), channel_id=1, source_target_pairs={{0,32},{32,64},{64,96},{96,128},{128,160},{160,192},{192,224},{224... | collective-permute-start | bytes 1572872 | tf_op jit(solution)/shard_map/ppermute | solution.py:15
  11.8 3.6 copy-start.4
  15.4 16.4 %copy-start.17 = (bf16[1,128,2048]{2,1,0:T(8,128)(2,1)S(1)}, bf16[1,128,2048]{2,1,0:T(8,128)(2,1)}, u32[]{:S(2)}) copy-start(bf16[1,128,2048]{2,1,0:T(8,128)(2,1)} %param.15) | copy-start | bytes 1572868
  15.4 20.7 %copy-start.12 = (s32[1,128,1]{1,2,0:T(1,128)S(1)}, s32[1,128,1]{1,2,0:T(1,128)}, u32[]{:S(2)}) copy-start(s32[1,128,1]{1,2,0:T(1,128)} %param.22) | copy-start | bytes 1540
  15.4 21.2 %copy-start.2 = (bf16[1,128,2048]{2,1,0:T(8,128)(2,1)S(1)}, bf16[1,128,2048]{2,1,0:T(8,128)(2,1)}, u32[]{:S(2)}) copy-start(bf16[1,128,2048]{2,1,0:T(8,128)(2,1)} %param.14) | copy-start | bytes 1572868
  15.4 21.9 %copy-start.9 = (f32[1,2048]{1,0:T(1,128)S(1)}, f32[1,2048]{1,0:T(1,128)}, u32[]{:S(2)}) copy-start(f32[1,2048]{1,0:T(1,128)} %param.16) | copy-start | bytes 24580
  15.4 153.0 %all-to-all-start = ((bf16[32,18,2048]{2,1,0:T(8,128)(2,1)}), bf16[32,18,2048]{2,1,0:T(8,128)(2,1)}, u32[]{:S(2)}, u32[]{:S(2)}) async-start(bf16[32,18,2048]{2,1,0:T(8,128)(2,1)} %bitcast.68), calls=%async_computation | async-start | bytes 6291456 | tf_op jit(solution)/shard_map/all_to_all | solution.py:133
  31.7 14.2 %collective-permute-start.1 = (bf16[1,128,2048]{2,1,0:T(8,128)(2,1)S(1)}, bf16[1,128,2048]{2,1,0:T(8,128)(2,1)S(1)}, u32[]{:S(2)}, u32[]{:S(2)}) collective-permute-start(bf16[1,128,2048]{2,1,0:T(8,128)(2,1)S(1)} %copy-done.17), channel_id=1, source_target_pairs={{0,480},{32,0},{64,32},{96,64},{128,96},{160,128},{192,160},{224,1... | collective-permute-start | bytes 1572872 | tf_op jit(solution)/shard_map/ppermute | solution.py:15
  37.2 10.0 %copy-start.14 = (f32[128]{0:T(128)}, f32[128]{0:T(128)S(1)}, u32[]{:S(2)}) copy-start(f32[128]{0:T(128)S(1)} %add_rsqrt_fusion) | copy-start | bytes 1540
  45.9 0.8 copy-start.7
  170.5 149.3 %all-to-all-start.2 = ((bf16[32,18,2048]{2,1,0:T(8,128)(2,1)}), bf16[32,18,2048]{2,1,0:T(8,128)(2,1)}, u32[]{:S(2)}, u32[]{:S(2)}) async-start(bf16[32,18,2048]{2,1,0:T(8,128)(2,1)} %bitcast.70), calls=%async_computation.2 | async-start | bytes 6291456 | tf_op jit(solution)/shard_map/all_to_all | solution.py:146
  321.8 149.0 %all-to-all-start.3 = ((bf16[32,18,2048]{2,1,0:T(8,128)(2,1)}), bf16[32,18,2048]{2,1,0:T(8,128)(2,1)}, u32[]{:S(2)}, u32[]{:S(2)}) async-start(bf16[32,18,2048]{2,1,0:T(8,128)(2,1)} %bitcast.69), calls=%async_computation.3 | async-start | bytes 6291456 | tf_op jit(solution)/shard_map/all_to_all | solution.py:145
  470.8 148.8 %all-to-all-start.1 = ((bf16[32,18,2048]{2,1,0:T(8,128)(2,1)}), bf16[32,18,2048]{2,1,0:T(8,128)(2,1)}, u32[]{:S(2)}, u32[]{:S(2)}) async-start(bf16[32,18,2048]{2,1,0:T(8,128)(2,1)} %reshape.192), calls=%async_computation.1 | async-start | bytes 6291456 | tf_op jit(solution)/shard_map/all_to_all | solution.py:131
  490.1 3.7 copy-start.8
  619.6 149.1 %all-to-all-start.4 = ((bf16[32,18,2048]{2,1,0:T(8,128)(2,1)}), bf16[32,18,2048]{2,1,0:T(8,128)(2,1)}, u32[]{:S(2)}, u32[]{:S(2)}) async-start(bf16[32,18,2048]{2,1,0:T(8,128)(2,1)} %reshape.198), calls=%async_computation.4 | async-start | bytes 6291456 | tf_op jit(solution)/shard_map/all_to_all | solution.py:143
  774.1 2.0 copy-start.10
  774.2 2.0 copy-start.13
  778.4 1.9 copy-start.1
  778.4 1.9 copy-start.3
  778.4 1.9 copy-start.11
  780.4 2.5 copy-start.5
  780.4 2.5 copy-start.6
  780.4 2.5 copy-start.15
  780.4 2.5 copy-start.16
where the time goes:
time: 792 us; the launch traced here: 784 us
  waiting for transfers between devices  638 us (81%)
  starting transfers between devices  73.8 us (9%)
  local copies, waits for them, and re-layouts  30.3 us (4%)
  matrix products  23.9 us (3%)
  other arithmetic  16.8 us (2%)
    all_to_all x1, waiting for transfers between devices, per_device(): lax.all_to_all(send_g, 'expert', split_axis=0, concat_axis=0, tiled=True)  137 us
    all_to_all x1, waiting for transfers between devices, per_device(): lax.all_to_all(backward_rows(lax.all_to_all(send_b, 'expert', split_axis=...  134 us
    all_to_all x1, waiting for transfers between devices, per_device(): lax.all_to_all(send_b, 'expert', split_axis=0, concat_axis=0, tiled=True)  122 us
    all_to_all x1, waiting for transfers between devices, per_device(): lax.all_to_all(send_f, 'expert', split_axis=0, concat_axis=0, tiled=True)  121 us
    all_to_all x1, waiting for transfers between devices, per_device(): lax.all_to_all(forward_rows(lax.all_to_all(send_f, 'expert', split_axis=0...  112 us
    all_to_all x1, starting transfers between devices, per_device(): lax.all_to_all(send_f, 'expert', split_axis=0, concat_axis=0, tiled=True)  16.3 us
  transfers between devices with their start and end apart: 7, of which 7 were waited for; matrix products, arithmetic and copies ran while one was open for 6% of the time, Pallas kernels for 0%

commit v1 on v0

v1 whole, which is shorter than its diff:
```python
import jax
import jax.numpy as jnp
from jax import lax
from jax.experimental import pallas as pl
from jax.experimental.pallas import tpu as pltpu
from jax.sharding import PartitionSpec as P

MESH = pl.DeviceIdType.MESH

SPLIT = 4
EXPERTS = 8
D = 2048
UNITS = 192
WIDE = UNITS * SPLIT
MAIN = 16
TAIL = 2
SOURCES = 16
ROWS = SOURCES * (MAIN + TAIL)
FIRST_TAIL = SOURCES * MAIN
RING = 16
BLOCKS = RING // SPLIT
TILE = 256

norm_eps = 1e-06

NT = (((1,), (1,)), ((), ()))


def passed_along(value, axis, steps):
    count = lax.axis_size(axis)
    pairs = [(source, (source + steps) % count) for source in range(count)]
    return lax.ppermute(value, axis, pairs)


def normalize(block_rows, gain_row):
    values = block_rows.astype(jnp.float32)
    inv_scale = lax.rsqrt(jnp.mean(values * values, axis=-1, keepdims=True) + norm_eps)
    return (values * inv_scale * gain_row, inv_scale)


def slot_chooser(routes):
    flat_routes = routes[:, 0]
    onehot = (flat_routes[:, None] == jnp.arange(EXPERTS, dtype=jnp.int32)[None, :]).astype(
        jnp.int32
    )
    before = jnp.cumsum(onehot, axis=0) - onehot
    slot_index = jnp.sum(before * onehot, axis=1)
    target = jnp.where(
        slot_index < MAIN,
        flat_routes * MAIN + slot_index,
        EXPERTS * MAIN + flat_routes * TAIL + slot_index - MAIN,
    )
    total = EXPERTS * (MAIN + TAIL)
    return (jnp.arange(total, dtype=jnp.int32)[:, None] == target[None, :]).astype(jnp.bfloat16)


def way(block, place, expert):
    there = expert % BLOCKS
    apart = lax.rem(there - block + BLOCKS, BLOCKS)
    low = place < 2
    member = jnp.where(
        apart == 0,
        jnp.where(low, 1, 2),
        jnp.where(apart == 1, 1, jnp.where(apart == 3, 2, jnp.where(low, 2, 1))),
    )
    odd = lax.rem(place, 2)
    kind = jnp.where(apart == 0, 6 + odd, jnp.where(apart == 2, 4 + odd, place))
    return (expert // BLOCKS) * RING + there * SPLIT + member, kind


def origin(block, place, slot):
    source_x = slot // 8
    kind = lax.rem(slot, 8)
    left = place == 1
    apart = jnp.where(kind < 4, jnp.where(left, 3, 1), jnp.where(kind < 6, 2, 0))
    source_place = jnp.where(
        kind < 4,
        kind,
        jnp.where(
            kind < 6,
            jnp.where(left, kind - 2, kind - 4),
            jnp.where(left, kind - 6, kind - 4),
        ),
    )
    source_block = lax.rem(block + apart, BLOCKS)
    return source_x * RING + source_block * SPLIT + source_place


def expert_kernel(
    f_main, f_tail, b_main, b_tail, g_main, g_tail, wg_in, wu_in, wd_in,
    of_main, of_tail, ob_main, ob_tail,
    xf, xft, xb, xbt, xg, xgt, wg, wu, wd, yf, yft, yb, ybt, hid_a, hid_b, tail_rows,
    w_local, w_send, w_recv, send_m, send_t, recv_m, recv_t, back_m, back_t, home_m, home_t,
):
    me = lax.axis_index("expert")
    x_lo = me // RING
    z = lax.rem(me, RING)
    block = z // SPLIT
    place = lax.rem(z, SPLIT)
    computing = jnp.logical_and(place >= 1, place <= 2)
    peer = me + 3 - 2 * place
    inner = jnp.where(place == 0, me + 1, me - 1)

    barrier = pltpu.get_barrier_semaphore()

    def greet(expert, carry):
        dest, _ = way(block, place, expert)

        @pl.when(dest != me)
        def _():
            pl.semaphore_signal(barrier, inc=1, device_id={"expert": dest}, device_id_type=MESH)

        return carry

    lax.fori_loop(0, EXPERTS, greet, 0)

    @pl.when(computing)
    def _():
        def greet_source(slot, carry):
            source = origin(block, place, slot)

            @pl.when(source != me)
            def _():
                pl.semaphore_signal(
                    barrier, inc=1, device_id={"expert": source}, device_id_type=MESH
                )

            return carry

        lax.fori_loop(0, SOURCES, greet_source, 0)
        pl.semaphore_signal(barrier, inc=1, device_id={"expert": peer}, device_id_type=MESH)
        pl.semaphore_wait(barrier, EXPERTS - 1 + SOURCES - 1 + 1)

    @pl.when(jnp.logical_not(computing))
    def _():
        pl.semaphore_wait(barrier, EXPERTS)

    weights = ((wg_in, wg), (wu_in, wu), (wd_in, wd))

    def share_rows(share):
        return pl.ds(pl.multiple_of(share * UNITS, UNITS), UNITS)

    def weight_copy(kind, source, share, where, device, passed):
        return pltpu.make_async_remote_copy(
            src_ref=source,
            dst_ref=weights[kind][1].at[share_rows(share)],
            send_sem=w_send.at[passed, kind],
            recv_sem=w_recv.at[where, kind],
            device_id={"expert": device},
            device_id_type=MESH,
        )

    for kind in range(3):
        own = weights[kind][0]

        @pl.when(computing)
        def _():
            weight_copy(kind, own, place, 0, peer, 0).start()
            pltpu.make_async_copy(own, weights[kind][1].at[share_rows(place)], w_local.at[kind]).start()

        @pl.when(jnp.logical_not(computing))
        def _():
            weight_copy(kind, own, place, 1, inner, 0).start()

    streams = (
        (f_main, f_tail, xf, xft),
        (b_main, b_tail, xb, xbt),
        (g_main, g_tail, xg, xgt),
    )

    def main_rows(index):
        return pl.ds(pl.multiple_of(index * MAIN, MAIN), MAIN)

    def send_stream(stream):
        main_in, tail_in, main_there, tail_there = streams[stream]

        def body(expert, carry):
            dest, kind = way(block, place, expert)
            slot = x_lo * 8 + kind
            pieces = (
                (main_in.at[main_rows(expert)], main_there.at[main_rows(slot)], send_m, recv_m),
                (tail_in.at[expert], tail_there.at[slot], send_t, recv_t),
            )
            for source, target, sent, got in pieces:

                @pl.when(dest == me)
                def _():
                    pltpu.make_async_copy(source, target, got.at[stream, slot]).start()

                @pl.when(dest != me)
                def _():
                    pltpu.make_async_remote_copy(
                        src_ref=source,
                        dst_ref=target,
                        send_sem=sent.at[stream, expert],
                        recv_sem=got.at[stream, slot],
                        device_id={"expert": dest},
                        device_id_type=MESH,
                    ).start()

            return carry

        lax.fori_loop(0, EXPERTS, body, 0)

    for stream in range(3):
        send_stream(stream)

    def wait_stream(stream):
        main_in, tail_in, main_there, tail_there = streams[stream]

        def body(slot, carry):
            pltpu.make_async_copy(
                main_in.at[main_rows(0)], main_there.at[main_rows(slot)], recv_m.at[stream, slot]
            ).wait()
            pltpu.make_async_copy(
                tail_in.at[0], tail_there.at[slot], recv_t.at[stream, slot]
            ).wait()
            return carry

        lax.fori_loop(0, SOURCES, body, 0)
        for slot in range(SOURCES):
            tail_rows[pl.ds(slot * TAIL, TAIL), :] = tail_there[slot].astype(jnp.float32)
        main_there[pl.ds(FIRST_TAIL, SOURCES * TAIL), :] = tail_rows[...].astype(jnp.bfloat16)

    def send_back(which, main_here, tail_here, main_home, tail_home):
        def body(slot, carry):
            source = origin(block, place, slot)
            expert = x_lo * BLOCKS + block
            pieces = (
                (main_here.at[main_rows(slot)], main_home.at[main_rows(expert)], back_m, home_m),
                (tail_here.at[slot], tail_home.at[expert], back_t, home_t),
            )
            for here, target, sent, got in pieces:

                @pl.when(source == me)
                def _():
                    pltpu.make_async_copy(here, target, got.at[which, expert]).start()

                @pl.when(source != me)
                def _():
                    pltpu.make_async_remote_copy(
                        src_ref=here,
                        dst_ref=target,
                        send_sem=sent.at[which, slot],
                        recv_sem=got.at[which, expert],
                        device_id={"expert": source},
                        device_id_type=MESH,
                    ).start()

            return carry

        lax.fori_loop(0, SOURCES, body, 0)

    def cols(step):
        return pl.ds(pl.multiple_of(step * TILE, TILE), TILE)

    def put_result(main_here, step, value):
        main_here[:, cols(step)] = value[:FIRST_TAIL].astype(jnp.bfloat16)
        tail_rows[:, cols(step)] = value[FIRST_TAIL:]

    def put_tails(tail_here):
        for slot in range(SOURCES):
            tail_here[slot] = tail_rows[pl.ds(slot * TAIL, TAIL), :].astype(jnp.bfloat16)

    def dot_nt(left, right):
        return lax.dot_general(left, right, NT, preferred_element_type=jnp.float32)

    def dot_nn(left, right):
        return jnp.dot(left, right, preferred_element_type=jnp.float32)

    @pl.when(computing)
    def _():
        outer_share = jnp.where(place == 1, 0, 3)
        for kind in range(3):
            held = weights[kind][1].at[share_rows(outer_share)]
            weight_copy(kind, held, outer_share, 1, inner, 0).wait_recv()
            weight_copy(kind, held, outer_share, 2, peer, 1).start()
        for kind in range(3):
            own = weights[kind][0]
            held = weights[kind][1].at[share_rows(place)]
            pltpu.make_async_copy(own, held, w_local.at[kind]).wait()
            far = weights[kind][1].at[share_rows(3 - place)]
            weight_copy(kind, far, 3 - place, 0, peer, 0).wait_recv()
            farther = weights[kind][1].at[share_rows(3 - outer_share)]
            weight_copy(kind, farther, 3 - outer_share, 2, peer, 1).wait_recv()

        wait_stream(0)

        def forward_hidden(step, carry):
            gate_pre = dot_nt(xf[...], wg[cols(step), :])
            up_pre = dot_nt(xf[...], wu[cols(step), :])
            hid_a[:, cols(step)] = (gate_pre * jax.nn.sigmoid(gate_pre) * up_pre).astype(
                jnp.bfloat16
            )
            return carry

        lax.fori_loop(0, WIDE // TILE, forward_hidden, 0)

        def forward_out(step, carry):
            put_result(yf, step, dot_nn(hid_a[...], wd[:, cols(step)]))
            return carry

        lax.fori_loop(0, D // TILE, forward_out, 0)
        put_tails(yft)
        send_back(0, yf, yft, of_main, of_tail)

        wait_stream(1)
        wait_stream(2)

        def backward_hidden(step, carry):
            gate_pre = dot_nt(xb[...], wg[cols(step), :])
            up_pre = dot_nt(xb[...], wu[cols(step), :])
            d_hidden = dot_nt(xg[...], wd[cols(step), :])
            sigma = jax.nn.sigmoid(gate_pre)
            hid_a[:, cols(step)] = (
                d_hidden * up_pre * (sigma * (1.0 + gate_pre * (1.0 - sigma)))
            ).astype(jnp.bfloat16)
            hid_b[:, cols(step)] = (d_hidden * (gate_pre * sigma)).astype(jnp.bfloat16)
            return carry

        lax.fori_loop(0, WIDE // TILE, backward_hidden, 0)

        def backward_out(step, carry):
            value = dot_nn(hid_a[...], wg[:, cols(step)]) + dot_nn(hid_b[...], wu[:, cols(step)])
            put_result(yb, step, value)
            return carry

        lax.fori_loop(0, D // TILE, backward_out, 0)
        put_tails(ybt)
        send_back(1, yb, ybt, ob_main, ob_tail)

    homes = ((yf, yft, of_main, of_tail), (yb, ybt, ob_main, ob_tail))
    for which in range(2):
        main_here, tail_here, main_home, tail_home = homes[which]

        def home(expert, carry):
            pltpu.make_async_copy(
                main_here.at[main_rows(0)], main_home.at[main_rows(expert)], home_m.at[which, expert]
            ).wait()
            pltpu.make_async_copy(
                tail_here.at[0], tail_home.at[expert], home_t.at[which, expert]
            ).wait()
            return carry

        lax.fori_loop(0, EXPERTS, home, 0)

    for stream in range(3):
        main_in, tail_in, main_there, tail_there = streams[stream]

        def left(expert, carry):
            dest, _ = way(block, place, expert)

            @pl.when(dest != me)
            def _():
                pltpu.make_async_copy(
                    main_in.at[main_rows(expert)], main_there.at[main_rows(0)],
                    send_m.at[stream, expert],
                ).wait()
                pltpu.make_async_copy(
                    tail_in.at[expert], tail_there.at[0], send_t.at[stream, expert]
                ).wait()

            return carry

        lax.fori_loop(0, EXPERTS, left, 0)

    for kind in range(3):
        weight_copy(kind, weights[kind][0], place, 0, inner, 0).wait_send()

    @pl.when(computing)
    def _():
        for kind in range(3):
            weight_copy(kind, weights[kind][0], place, 2, peer, 1).wait_send()
        for which in range(2):
            main_here, tail_here, main_home, tail_home = homes[which]

            def gone(slot, carry):
                source = origin(block, place, slot)

                @pl.when(source != me)
                def _():
                    pltpu.make_async_copy(
                        main_here.at[main_rows(slot)], main_home.at[main_rows(0)],
                        back_m.at[which, slot],
                    ).wait()
                    pltpu.make_async_copy(
                        tail_here.at[slot], tail_home.at[0], back_t.at[which, slot]
                    ).wait()

                return carry

            lax.fori_loop(0, SOURCES, gone, 0)


def run_experts(main_f, tail_f, main_b, tail_b, main_g, tail_g, gate_w, up_w, down_w):
    bf16 = jnp.bfloat16
    vmem = pl.BlockSpec(memory_space=pltpu.VMEM)
    dma = pltpu.SemaphoreType.DMA
    rows_in = pltpu.VMEM((ROWS, D), bf16)
    tails_in = pltpu.VMEM((SOURCES, TAIL, D), bf16)
    weight = pltpu.VMEM((WIDE, D), bf16)
    main_out = pltpu.VMEM((FIRST_TAIL, D), bf16)
    home_main = jax.ShapeDtypeStruct((EXPERTS * MAIN, D), bf16)
    home_tail = jax.ShapeDtypeStruct((EXPERTS, TAIL, D), bf16)
    return pl.pallas_call(
        expert_kernel,
        out_shape=(home_main, home_tail, home_main, home_tail),
        in_specs=[vmem] * 9,
        out_specs=(vmem,) * 4,
        scratch_shapes=[
            rows_in, tails_in, rows_in, tails_in, rows_in, tails_in,
            weight, weight, weight,
            main_out, tails_in, main_out, tails_in,
            pltpu.VMEM((ROWS, WIDE), bf16), pltpu.VMEM((ROWS, WIDE), bf16),
            pltpu.VMEM((SOURCES * TAIL, D), jnp.float32),
            dma((3,)), dma((2, 3)), dma((3, 3)),
            dma((3, EXPERTS)), dma((3, EXPERTS)), dma((3, SOURCES)), dma((3, SOURCES)),
            dma((2, SOURCES)), dma((2, SOURCES)), dma((2, EXPERTS)), dma((2, EXPERTS)),
        ],
        compiler_params=pltpu.CompilerParams(
            collective_id=0, has_side_effects=True, vmem_limit_bytes=48 * 1024 * 1024
        ),
        name="experts",
    )(main_f, tail_f, main_b, tail_b, main_g, tail_g, gate_w, up_w, down_w)


def split_rows(packed):
    main = packed[: EXPERTS * MAIN]
    return main, packed[EXPERTS * MAIN :].reshape(EXPERTS, TAIL, D)


def brought_home(chooser, main, tail, gates):
    rows = jnp.concatenate([main, tail.reshape(EXPERTS * TAIL, D)], axis=0)
    picked = lax.dot_general(
        chooser, rows, (((0,), (0,)), ((), ())), preferred_element_type=jnp.float32
    )
    return picked * gates


def per_device(
    act_in,
    saved_in,
    grad_in,
    norm_gain,
    w_gate,
    w_up,
    w_down,
    routes_fwd,
    gates_fwd,
    routes_bwd,
    gates_bwd,
):
    gain_row = norm_gain[0]
    incoming = passed_along(act_in, "section", 1)[0]
    upstream = passed_along(grad_in, "section", -1)[0]
    n_fwd = normalize(incoming, gain_row)[0].astype(jnp.bfloat16)
    values_b, inv_scale = normalize(saved_in[0], gain_row)
    n_bwd = values_b.astype(jnp.bfloat16)
    chooser_f = slot_chooser(routes_fwd[0])
    chooser_b = slot_chooser(routes_bwd[0])

    def packed(chooser, values):
        return split_rows(
            jnp.dot(chooser, values, preferred_element_type=jnp.float32).astype(jnp.bfloat16)
        )

    main_f, tail_f = packed(chooser_f, n_fwd)
    main_b, tail_b = packed(chooser_b, n_bwd)
    main_g, tail_g = packed(chooser_b, upstream)
    f_main, f_tail, b_main, b_tail = run_experts(
        main_f, tail_f, main_b, tail_b, main_g, tail_g, w_gate[0].T, w_up[0].T, w_down[0]
    )
    mixed = brought_home(chooser_f, f_main, f_tail, gates_fwd[0])
    act_out = (incoming.astype(jnp.float32) + mixed).astype(jnp.bfloat16)
    d_norm = brought_home(chooser_b, b_main, b_tail, gates_bwd[0])
    scaled = d_norm * gain_row
    base = saved_in[0].astype(jnp.float32)
    d_input = inv_scale * (
        scaled - base * inv_scale * inv_scale * jnp.mean(scaled * base, axis=-1, keepdims=True)
    )
    grad_out = (upstream.astype(jnp.float32) + d_input).astype(jnp.bfloat16)
    return (act_out[None], grad_out[None])


def solution(mesh):
    in_specs = (
        P("section", "expert", None),
        P("section", "expert", None),
        P("section", "expert", None),
        P("section", None),
        P("section", None, "expert"),
        P("section", None, "expert"),
        P("section", "expert", None),
        P("section", "expert", None),
        P("section", "expert", None),
        P("section", "expert", None),
        P("section", "expert", None),
    )
    out_specs = (P("section", "expert", None), P("section", "expert", None))
    return jax.shard_map(
        per_device, mesh=mesh, in_specs=in_specs, out_specs=out_specs, check_vma=False
    )
```

time: 792 us -> 262 us (0.33)
  waiting for transfers between devices: 638 us -> 5.72 us
  Pallas kernels: 0 us -> 232 us
  starting transfers between devices: 73.8 us -> 6.53 us
  local copies, waits for them, and re-layouts: 30.3 us -> 4.59 us
  matrix products: 23.9 us -> 5.04 us
  other arithmetic: 16.8 us -> 5.44 us
    all_to_all x5 -> x0, waiting for transfers between devices: 626 us -> none  [the longest x1 137 us: per_device(): lax.all_to_all(send_g, 'expert', split_axis=0, concat_axis=0, tiled=True)]
    pallas_call x0 -> x1, Pallas kernels: none -> 232 us  [run_experts(): pl.pallas_call(expert_kernel, out_shape=(home_main, home_tail, home_main,...]
    all_to_all x5 -> x0, starting transfers between devices: 64.7 us -> none  [the longest x1 16.3 us: per_device(): lax.all_to_all(send_f, 'expert', split_axis=0, concat_axis=0, tiled=True)]
    dot_general x8 -> x5, matrix products: 23.9 us -> 5.04 us  [the longest x2 2.9 us: brought_home(): lax.dot_general(chooser, rows, (((0,), (0,)), ((), ())), preferred_elemen...]
    reshape x7 -> x5, local copies, waits for them, and re-layouts: 18.7 us -> 0.22 us  [the longest x3 0.16 us: split_rows(): return (main, packed[EXPERTS * MAIN:].reshape(EXPERTS, TAIL, D))]
    reduce_sum x3 -> x0, other arithmetic: 8.19 us -> none  [the longest x2 6.44 us: combine(): jnp.sum(returned.reshape(experts, SPLIT, capacity, row_width).astype(jnp....]
  transfers between devices with their start and end apart: 7 -> 2, of which waited for: 7 -> 2; matrix products, arithmetic and copies ran while one was open for 6% -> 2% of each run, Pallas kernels for 0% -> 0%
where the time goes in v1:
time: 262 us; the launch traced here: 260 us
  Pallas kernels  232 us (89%)
  starting transfers between devices  6.53 us (2%)
  waiting for transfers between devices  5.72 us (2%)
  other arithmetic  5.44 us (2%)
  matrix products  5.04 us (2%)
  local copies, waits for them, and re-layouts  4.59 us (2%)
    pallas_call x1, Pallas kernels, run_experts(): pl.pallas_call(expert_kernel, out_shape=(home_main, home_tail, home_main,...  232 us
    ppermute x2, starting transfers between devices, passed_along(): return lax.ppermute(value, axis, pairs)  6.53 us
    ppermute x2, waiting for transfers between devices, passed_along(): return lax.ppermute(value, axis, pairs)  5.72 us
  transfers between devices with their start and end apart: 2, of which 2 were waited for; matrix products, arithmetic and copies ran while one was open for 2% of the time, Pallas kernels for 0%

profile of v1, /device:TPU:7, one launch (start us, length us, event | category | flops | bytes accessed | tf_op | source)
XLA Modules:
  0.0 260.3 jit_solution(9995409571409120982)
XLA Ops:
  0.6 4.6 %collective-permute-start = (bf16[1,128,2048]{2,1,0:T(8,128)(2,1)}, bf16[1,128,2048]{2,1,0:T(8,128)(2,1)S(1)}, u32[]{:S(2)}, u32[]{:S(2)}) collective-permute-start(bf16[1,128,2048]{2,1,0:T(8,128)(2,1)} %param.11), channel_id=1, source_target_pairs={{0,32},{32,64},{64,96},{96,128},{128,160},{160,192},{192,224},{224... | collective-permute-start | bytes 1572872 | tf_op jit(solution)/shard_map/ppermute | solution.py:32
  5.2 1.9 collective-permute-start.1
  7.2 1.2 fusion.15
  8.4 0.7 fusion.33
  9.2 0.2 reduce_window_sum.18
  9.3 0.8 select_reduce_fusion
  10.2 0.7 compare_select_fusion
  10.8 1.4 convolution_convert_fusion.1
  12.3 0.0 copy-start.12
  12.4 0.0 copy-done.13
  12.4 0.1 fusion.34
  12.5 0.2 reduce_window_sum.17
  12.6 0.1 reshape.82.b_tail
  12.7 0.2 select_reduce_fusion.1
  12.9 1.0 collective-permute-done
  13.9 0.2 fusion.12
  14.1 0.0 copy-done.12
  14.1 0.4 convolution_convert_fusion.2
  14.5 0.2 copy-done.8
  14.7 0.0 copy-start
  14.7 0.0 copy-start.1
  14.8 4.7 %collective-permute-done.1 = bf16[1,128,2048]{2,1,0:T(8,128)(2,1)S(1)} collective-permute-done((bf16[1,128,2048]{2,1,0:T(8,128)(2,1)}, bf16[1,128,2048]{2,1,0:T(8,128)(2,1)S(1)}, u32[]{:S(2)}, u32[]{:S(2)}) %collective-permute-start.1) | collective-permute-done | bytes 524320 | tf_op jit(solution)/shard_map/ppermute | solution.py:32
  19.5 0.3 convolution_convert_fusion
  19.8 0.0 copy-done.7
  19.8 0.5 copy-done.10
  20.3 0.8 slice-done
  21.1 0.1 reshape.81.f_tail
  21.2 0.1 reshape.83.g_tail
  21.2 0.0 copy-done
  21.2 0.0 copy-done.1
  21.2 0.0 copy-start.2
  21.3 1.1 copy-done.2
  22.4 232.1 %experts.1 = (bf16[128,2048]{1,0:T(8,128)(2,1)S(1)}, bf16[8,2,2048]{2,1,0:T(2,128)(2,1)S(1)}, bf16[128,2048]{1,0:T(8,128)(2,1)S(1)}, bf16[8,2,2048]{2,1,0:T(2,128)(2,1)S(1)}) custom-call(bf16[128,2048]{1,0:T(8,128)(2,1)S(1)} %slice.24.f_main, bf16[8,2,2048]{2,1,0:T(2,128)(2,1)S(1)} %reshape.81.f_tail, bf16[128,2048]{1,0:T(8,128)(2,1)S(1)} %slice.26.b_main, ...), custom_call_target="tpu_custom_call" | custom-call | tf_op jit(solution)/shard_map/experts/pallas_call | solution.py:405
  254.4 0.0 copy-start.3
  254.5 0.8 copy-done.3
  255.2 0.8 copy-done.5
  256.1 0.0 copy-done.14
  256.1 0.0 copy-start.6
  256.1 0.0 copy-start.11
  256.1 1.7 fusion.16
  257.9 0.0 copy-done.6
  257.9 0.0 copy-done.11
  257.9 0.0 copy-start.4
  257.9 0.0 copy-start.9
  257.9 0.0 copy-start.15
  257.9 1.2 fusion.24
  259.1 0.0 copy-done.9
  259.1 1.1 fusion.3
  (20 shorter events, 0.2 us)
Async XLA Ops:
  0.6 13.3 %collective-permute-start = (bf16[1,128,2048]{2,1,0:T(8,128)(2,1)}, bf16[1,128,2048]{2,1,0:T(8,128)(2,1)S(1)}, u32[]{:S(2)}, u32[]{:S(2)}) collective-permute-start(bf16[1,128,2048]{2,1,0:T(8,128)(2,1)} %param.11), channel_id=1, source_target_pairs={{0,32},{32,64},{64,96},{96,128},{128,160},{160,192},{192,224},{224... | collective-permute-start | bytes 1572872 | tf_op jit(solution)/shard_map/ppermute | solution.py:32
  5.2 14.2 %collective-permute-start.1 = (bf16[1,128,2048]{2,1,0:T(8,128)(2,1)}, bf16[1,128,2048]{2,1,0:T(8,128)(2,1)S(1)}, u32[]{:S(2)}, u32[]{:S(2)}) collective-permute-start(bf16[1,128,2048]{2,1,0:T(8,128)(2,1)} %param.13), channel_id=1, source_target_pairs={{0,480},{32,0},{64,32},{96,64},{128,96},{160,128},{192,160},{224,1... | collective-permute-start | bytes 1572872 | tf_op jit(solution)/shard_map/ppermute | solution.py:32
  10.8 1.5 copy-start.13
  12.3 1.8 copy-start.12
  13.9 0.8 copy-start.8
  14.7 5.1 %copy-start.7 = (bf16[144,2048]{1,0:T(8,128)(2,1)}, bf16[144,2048]{1,0:T(8,128)(2,1)S(1)}, u32[]{:S(2)}) copy-start(bf16[144,2048]{1,0:T(8,128)(2,1)S(1)} %convolution_convert_fusion.2) | copy-start | bytes 1769476
  14.7 6.5 %copy-start = (bf16[1,2048,192]{1,2,0:T(8,128)(2,1)S(1)}, bf16[1,2048,192]{1,2,0:T(8,128)(2,1)}, u32[]{:S(2)}) copy-start(bf16[1,2048,192]{1,2,0:T(8,128)(2,1)} %param.15) | copy-start | bytes 2359300
  14.7 6.5 %copy-start.1 = (bf16[1,2048,192]{1,2,0:T(8,128)(2,1)S(1)}, bf16[1,2048,192]{1,2,0:T(8,128)(2,1)}, u32[]{:S(2)}) copy-start(bf16[1,2048,192]{1,2,0:T(8,128)(2,1)} %param.16) | copy-start | bytes 2359300
  19.5 0.8 copy-start.10
  20.3 0.8 slice-start
  21.2 1.1 copy-start.2
  22.4 233.7 %copy-start.14 = (f32[1,128,1]{1,2,0:T(1,128)S(1)}, f32[1,128,1]{1,2,0:T(1,128)}, u32[]{:S(2)}) copy-start(f32[1,128,1]{1,2,0:T(1,128)} %param.21) | copy-start | bytes 1540
  254.4 0.8 copy-start.3
  255.2 0.8 copy-start.5
  256.1 1.8 copy-start.6
  256.1 1.8 copy-start.11
  257.9 1.2 copy-start.4
  257.9 1.2 copy-start.9
  257.9 1.2 copy-start.15

commit v2 on v1

v2 whole, which is shorter than its diff:
```python
import jax
import jax.numpy as jnp
from jax import lax
from jax.experimental import pallas as pl
from jax.experimental.pallas import tpu as pltpu
from jax.sharding import PartitionSpec as P

MESH = pl.DeviceIdType.MESH

SPLIT = 4
EXPERTS = 8
D = 2048
TOK = 128
UNITS = 192
WIDE = UNITS * SPLIT
MAIN = 16
TAIL = 2
PACKED = EXPERTS * (MAIN + TAIL)
EDGE_SLOTS = 14
SLOTS = 18
FIRST_TAIL = SLOTS * MAIN
TAIL_ROWS = SLOTS * TAIL
ROWS = 336
RING = 16
BLOCKS = RING // SPLIT
TILE = 256

norm_eps = 1e-06

NT = (((1,), (1,)), ((), ()))


def way(block, place, there):
    apart = lax.rem(there - block + BLOCKS, BLOCKS)
    low = place < 2
    to_edge = jnp.logical_or(
        apart == 1,
        jnp.logical_or(
            jnp.logical_and(apart == 2, place >= 2), jnp.logical_and(apart == 0, place == 0)
        ),
    )
    kind = jnp.where(
        apart == 0,
        jnp.where(place == 0, 6, 5 + place),
        jnp.where(apart == 2, jnp.where(low, 4 + place, 2 + place), place),
    )
    return jnp.where(to_edge, 0, 2), kind


def origin(block, place, slot):
    edge = place == 0
    stride = jnp.where(edge, EDGE_SLOTS // 2, SLOTS // 2)
    source_x = jnp.where(slot >= stride, 1, 0)
    kind = slot - source_x * stride
    apart = jnp.where(kind < 4, jnp.where(edge, 3, 1), jnp.where(kind < 6, 2, 0))
    source_place = jnp.where(
        kind < 4,
        kind,
        jnp.where(
            kind < 6,
            jnp.where(edge, kind - 2, kind - 4),
            jnp.where(edge, 0, kind - 5),
        ),
    )
    return source_x, lax.rem(block + apart, BLOCKS), source_place


def relay_kernel(
    act_in, saved_in, grad_in, gain, wg_in, wu_in, wd_in, routes_f, gates_f, routes_b, gates_b,
    act_out, grad_out,
    x_new, dy, f_main, f_tail, b_main, b_tail, g_main, g_tail,
    home_f, home_ft, home_b, home_bt, scaled,
    xf, xft, xb, xbt, xg, xgt, wg, wu, wd, yf, yft, yb, ybt, hid_a, hid_b, tail_rows, own_tails,
    hop_send, hop_recv, w_local, w_send, w_recv,
    send_m, send_t, recv_m, recv_t, back_m, back_t, home_m, home_ts,
):
    me = lax.axis_index("expert")
    section = lax.axis_index("section")
    sections = lax.axis_size("section")
    after = lax.rem(section + 1, sections)
    ahead = lax.rem(section + sections - 1, sections)
    mirrored = lax.rem(section, 2) == 1
    x_lo = me // RING
    z = lax.rem(me, RING)
    turned = jnp.where(mirrored, RING - 1 - z, z)
    block = turned // SPLIT
    place = lax.rem(turned, SPLIT)
    edge = place == 0
    middle = place == 2
    computing = jnp.logical_or(edge, middle)
    slots = jnp.where(edge, EDGE_SLOTS, SLOTS)

    def device(x, its_block, its_place):
        along = its_block * SPLIT + its_place
        return x * RING + jnp.where(mirrored, RING - 1 - along, along)

    def neighbour(its_place):
        return device(x_lo, block, its_place)

    def expert_row(x, its_block):
        return x * BLOCKS + jnp.where(mirrored, BLOCKS - 1 - its_block, its_block)

    own_expert = expert_row(x_lo, block)

    def target_of(number):
        x = number // BLOCKS
        there = lax.rem(number, BLOCKS)
        member, kind = way(block, place, there)
        slot = x_lo * jnp.where(member == 0, EDGE_SLOTS // 2, SLOTS // 2) + kind
        return device(x, there, member), slot, expert_row(x, there)

    def source_of(slot):
        return device(*origin(block, place, slot))

    barrier = pltpu.get_barrier_semaphore()

    def signal(name, index):
        pl.semaphore_signal(barrier, inc=1, device_id={name: index}, device_id_type=MESH)

    signal("section", after)
    signal("section", ahead)

    def greet(number, carry):
        dest, _, _ = target_of(number)

        @pl.when(dest != me)
        def _():
            signal("expert", dest)

        return carry

    lax.fori_loop(0, EXPERTS, greet, 0)

    @pl.when(computing)
    def _():
        def greet_source(slot, carry):
            source = source_of(slot)

            @pl.when(source != me)
            def _():
                signal("expert", source)

            return carry

        lax.fori_loop(0, slots, greet_source, 0)

    @pl.when(edge)
    def _():
        signal("expert", neighbour(1))
        signal("expert", neighbour(2))

    @pl.when(jnp.logical_or(place == 1, middle))
    def _():
        signal("expert", neighbour(0))

    def one_hots(routes):
        down = lax.broadcasted_iota(jnp.int32, (TOK, TOK), 0)
        across = lax.broadcasted_iota(jnp.int32, (TOK, TOK), 1)
        row = routes[...].astype(jnp.float32)
        rows = jnp.broadcast_to(row, (TOK, TOK))
        column = jnp.sum(jnp.where(down == across, rows, 0.0), axis=1, keepdims=True)
        same = rows == column
        slot_row = jnp.sum(jnp.where(jnp.logical_and(same, down < across), 1.0, 0.0), axis=0, keepdims=True)
        slot_column = jnp.sum(jnp.where(jnp.logical_and(same, across < down), 1.0, 0.0), axis=1, keepdims=True)

        def packed_row(expert, slot):
            return jnp.where(
                slot < MAIN, expert * MAIN + slot, EXPERTS * MAIN + expert * TAIL + slot - MAIN
            ).astype(jnp.int32)

        pick_in = lax.broadcasted_iota(jnp.int32, (PACKED, TOK), 0) == packed_row(row, slot_row)
        pick_out = lax.broadcasted_iota(jnp.int32, (TOK, PACKED), 1) == packed_row(column, slot_column)
        return (
            jnp.where(pick_in, 1.0, 0.0).astype(jnp.bfloat16),
            jnp.where(pick_out, 1.0, 0.0).astype(jnp.bfloat16),
        )

    def as_column(row_ref):
        down = lax.broadcasted_iota(jnp.int32, (TOK, TOK), 0)
        across = lax.broadcasted_iota(jnp.int32, (TOK, TOK), 1)
        rows = jnp.broadcast_to(row_ref[...], (TOK, TOK))
        return jnp.sum(jnp.where(down == across, rows, 0.0), axis=1, keepdims=True)

    def inverse_scale(rows):
        values = rows[...].astype(jnp.float32)
        return lax.rsqrt(jnp.mean(values * values, axis=-1, keepdims=True) + norm_eps)

    def static_cols(step):
        return slice(step * TILE, (step + 1) * TILE)

    def pack(chooser, rows, inv_scale, main, tail):
        for step in range(D // TILE):
            part = rows[:, static_cols(step)]
            if inv_scale is not None:
                part = (part.astype(jnp.float32) * inv_scale * gain[:, static_cols(step)]).astype(
                    jnp.bfloat16
                )
            value = jnp.dot(chooser, part, preferred_element_type=jnp.float32)
            main[:, static_cols(step)] = value[: EXPERTS * MAIN].astype(jnp.bfloat16)
            own_tails[:, static_cols(step)] = value[EXPERTS * MAIN :]
        for expert in range(EXPERTS):
            tail[expert] = own_tails[expert * TAIL : (expert + 1) * TAIL, :].astype(jnp.bfloat16)

    chooser_b, chosen_b = one_hots(routes_b)
    inv_b = inverse_scale(saved_in)
    pack(chooser_b, saved_in, inv_b, b_main, b_tail)

    pl.semaphore_wait(
        barrier,
        jnp.where(edge, 24, jnp.where(middle, 27, jnp.where(place == 1, 11, 10))),
    )

    weights = ((wg_in, wg), (wu_in, wu), (wd_in, wd))

    def share_rows(share):
        return pl.ds(pl.multiple_of(share * UNITS, UNITS), UNITS)

    def weight_copy(kind, source, share, sent, dest):
        return pltpu.make_async_remote_copy(
            src_ref=source,
            dst_ref=weights[kind][1].at[share_rows(share)],
            send_sem=w_send.at[sent, kind],
            recv_sem=w_recv.at[share, kind],
            device_id={"expert": dest},
            device_id_type=MESH,
        )

    def hop(source, target, number, there):
        return pltpu.make_async_remote_copy(
            src_ref=source,
            dst_ref=target,
            send_sem=hop_send.at[number],
            recv_sem=hop_recv.at[number],
            device_id={"section": there},
            device_id_type=MESH,
        )

    hop_act = hop(act_in, x_new, 0, after)
    hop_grad = hop(grad_in, dy, 1, ahead)
    hop_act.start()
    hop_grad.start()

    for kind in range(3):
        own = weights[kind][0]

        @pl.when(edge)
        def _():
            weight_copy(kind, own, 0, 0, neighbour(2)).start()

        @pl.when(place == 1)
        def _():
            weight_copy(kind, own, 1, 0, neighbour(0)).start()
            weight_copy(kind, own, 1, 1, neighbour(2)).start()

        @pl.when(middle)
        def _():
            weight_copy(kind, own, 2, 0, neighbour(0)).start()

        @pl.when(place == 3)
        def _():
            weight_copy(kind, own, 3, 0, neighbour(2)).start()

        @pl.when(computing)
        def _():
            pltpu.make_async_copy(
                own, weights[kind][1].at[share_rows(place)], w_local.at[kind]
            ).start()

    streams = (
        (f_main, f_tail, xf, xft),
        (b_main, b_tail, xb, xbt),
        (g_main, g_tail, xg, xgt),
    )

    def main_rows(index):
        return pl.ds(pl.multiple_of(index * MAIN, MAIN), MAIN)

    def send_stream(stream):
        main_in, tail_in, main_there, tail_there = streams[stream]

        def body(number, carry):
            dest, slot, expert = target_of(number)
            pieces = (
                (main_in.at[main_rows(expert)], main_there.at[main_rows(slot)], send_m, recv_m),
                (tail_in.at[expert], tail_there.at[slot], send_t, recv_t),
            )
            for source, target, sent, got in pieces:

                @pl.when(dest == me)
                def _():
                    pltpu.make_async_copy(source, target, got.at[stream, slot]).start()

                @pl.when(dest != me)
                def _():
                    pltpu.make_async_remote_copy(
                        src_ref=source,
                        dst_ref=target,
                        send_sem=sent.at[stream, number],
                        recv_sem=got.at[stream, slot],
                        device_id={"expert": dest},
                        device_id_type=MESH,
                    ).start()

            return carry

        lax.fori_loop(0, EXPERTS, body, 0)

    send_stream(1)

    chooser_f, chosen_f = one_hots(routes_f)
    hop_act.wait_recv()
    pack(chooser_f, x_new, inverse_scale(x_new), f_main, f_tail)
    send_stream(0)

    hop_grad.wait_recv()
    pack(chooser_b, dy, None, g_main, g_tail)
    send_stream(2)

    def wait_stream(stream):
        main_in, tail_in, main_there, tail_there = streams[stream]

        def body(slot, carry):
            pltpu.make_async_copy(
                main_in.at[main_rows(0)], main_there.at[main_rows(slot)], recv_m.at[stream, slot]
            ).wait()
            pltpu.make_async_copy(
                tail_in.at[0], tail_there.at[slot], recv_t.at[stream, slot]
            ).wait()
            return carry

        lax.fori_loop(0, slots, body, 0)
        for slot in range(SLOTS):
            tail_rows[slot * TAIL : (slot + 1) * TAIL, :] = tail_there[slot].astype(jnp.float32)
        main_there[FIRST_TAIL:ROWS, :] = tail_rows[...].astype(jnp.bfloat16)

    def send_back(which, main_here, tail_here, main_home, tail_home):
        def body(slot, carry):
            source = source_of(slot)
            pieces = (
                (main_here.at[main_rows(slot)], main_home.at[main_rows(own_expert)], back_m, home_m),
                (tail_here.at[slot], tail_home.at[own_expert], back_t, home_ts),
            )
            for here, target, sent, got in pieces:

                @pl.when(source == me)
                def _():
                    pltpu.make_async_copy(here, target, got.at[which, own_expert]).start()

                @pl.when(source != me)
                def _():
                    pltpu.make_async_remote_copy(
                        src_ref=here,
                        dst_ref=target,
                        send_sem=sent.at[which, slot],
                        recv_sem=got.at[which, own_expert],
                        device_id={"expert": source},
                        device_id_type=MESH,
                    ).start()

            return carry

        lax.fori_loop(0, slots, body, 0)

    def cols(step):
        return pl.ds(pl.multiple_of(step * TILE, TILE), TILE)

    def put_result(main_here, step, value):
        main_here[:, cols(step)] = value[:FIRST_TAIL].astype(jnp.bfloat16)
        tail_rows[:, cols(step)] = value[FIRST_TAIL:]

    def put_tails(tail_here):
        for slot in range(SLOTS):
            tail_here[slot] = tail_rows[slot * TAIL : (slot + 1) * TAIL, :].astype(jnp.bfloat16)

    def dot_nt(left, right):
        return lax.dot_general(left, right, NT, preferred_element_type=jnp.float32)

    def dot_nn(left, right):
        return jnp.dot(left, right, preferred_element_type=jnp.float32)

    @pl.when(middle)
    def _():
        for kind in range(3):
            held = weights[kind][1].at[share_rows(3)]
            weight_copy(kind, held, 3, 0, neighbour(0)).wait_recv()
            weight_copy(kind, held, 3, 1, neighbour(0)).start()

    @pl.when(computing)
    def _():
        for kind in range(3):
            own = weights[kind][0]
            held = weights[kind][1].at[share_rows(place)]
            pltpu.make_async_copy(own, held, w_local.at[kind]).wait()
            weight_copy(kind, held, 1, 0, neighbour(0)).wait_recv()
            weight_copy(kind, held, jnp.where(edge, 2, 0), 0, neighbour(0)).wait_recv()

        @pl.when(edge)
        def _():
            for kind in range(3):
                held = weights[kind][1].at[share_rows(3)]
                weight_copy(kind, held, 3, 0, neighbour(0)).wait_recv()

        wait_stream(0)

        def forward_hidden(step, carry):
            gate_pre = dot_nt(xf[...], wg[cols(step), :])
            up_pre = dot_nt(xf[...], wu[cols(step), :])
            hid_a[:, cols(step)] = (gate_pre * jax.nn.sigmoid(gate_pre) * up_pre).astype(
                jnp.bfloat16
            )
            return carry

        lax.fori_loop(0, WIDE // TILE, forward_hidden, 0)

        def forward_out(step, carry):
            put_result(yf, step, dot_nn(hid_a[...], wd[:, cols(step)]))
            return carry

        lax.fori_loop(0, D // TILE, forward_out, 0)
        put_tails(yft)
        send_back(0, yf, yft, home_f, home_ft)

        wait_stream(1)
        wait_stream(2)

        def backward_hidden(step, carry):
            gate_pre = dot_nt(xb[...], wg[cols(step), :])
            up_pre = dot_nt(xb[...], wu[cols(step), :])
            d_hidden = dot_nt(xg[...], wd[cols(step), :])
            sigma = jax.nn.sigmoid(gate_pre)
            hid_a[:, cols(step)] = (
                d_hidden * up_pre * (sigma * (1.0 + gate_pre * (1.0 - sigma)))
            ).astype(jnp.bfloat16)
            hid_b[:, cols(step)] = (d_hidden * (gate_pre * sigma)).astype(jnp.bfloat16)
            return carry

        lax.fori_loop(0, WIDE // TILE, backward_hidden, 0)

        def backward_out(step, carry):
            value = dot_nn(hid_a[...], wg[:, cols(step)]) + dot_nn(hid_b[...], wu[:, cols(step)])
            put_result(yb, step, value)
            return carry

        lax.fori_loop(0, D // TILE, backward_out, 0)
        put_tails(ybt)
        send_back(1, yb, ybt, home_b, home_bt)

    homes = ((yf, yft, home_f, home_ft), (yb, ybt, home_b, home_bt))

    def wait_home(which):
        main_here, tail_here, main_home, tail_home = homes[which]

        def body(expert, carry):
            pltpu.make_async_copy(
                main_here.at[main_rows(0)], main_home.at[main_rows(expert)], home_m.at[which, expert]
            ).wait()
            pltpu.make_async_copy(
                tail_here.at[0], tail_home.at[expert], home_ts.at[which, expert]
            ).wait()
            return carry

        lax.fori_loop(0, EXPERTS, body, 0)
        for expert in range(EXPERTS):
            own_tails[expert * TAIL : (expert + 1) * TAIL, :] = tail_home[expert].astype(jnp.float32)
        main_home[EXPERTS * MAIN :, :] = own_tails[...].astype(jnp.bfloat16)

    wait_home(0)
    gate_f = as_column(gates_f)
    for step in range(D // TILE):
        part = static_cols(step)
        mixed = dot_nn(chosen_f, home_f[:, part]) * gate_f
        act_out[:, part] = (x_new[:, part].astype(jnp.float32) + mixed).astype(jnp.bfloat16)

    wait_home(1)
    gate_b = as_column(gates_b)
    total = jnp.zeros((TOK, 1), jnp.float32)
    for step in range(D // TILE):
        part = static_cols(step)
        value = dot_nn(chosen_b, home_b[:, part]) * gate_b * gain[:, part]
        scaled[:, part] = value
        total = total + jnp.sum(
            value * saved_in[:, part].astype(jnp.float32), axis=-1, keepdims=True
        )
    inv_scale = inverse_scale(saved_in)
    fold = inv_scale * inv_scale * (total / D)
    for step in range(D // TILE):
        part = static_cols(step)
        d_input = inv_scale * (scaled[:, part] - saved_in[:, part].astype(jnp.float32) * fold)
        grad_out[:, part] = (dy[:, part].astype(jnp.float32) + d_input).astype(jnp.bfloat16)

    hop_act.wait_send()
    hop_grad.wait_send()

    for stream in range(3):
        main_in, tail_in, main_there, tail_there = streams[stream]

        def left(number, carry):
            dest, _, expert = target_of(number)

            @pl.when(dest != me)
            def _():
                pltpu.make_async_copy(
                    main_in.at[main_rows(expert)], main_there.at[main_rows(0)],
                    send_m.at[stream, number],
                ).wait()
                pltpu.make_async_copy(
                    tail_in.at[expert], tail_there.at[0], send_t.at[stream, number]
                ).wait()

            return carry

        lax.fori_loop(0, EXPERTS, left, 0)

    for kind in range(3):
        weight_copy(kind, weights[kind][0], 0, 0, neighbour(0)).wait_send()

    @pl.when(jnp.logical_or(place == 1, middle))
    def _():
        for kind in range(3):
            weight_copy(kind, weights[kind][0], 0, 1, neighbour(0)).wait_send()

    @pl.when(computing)
    def _():
        for which in range(2):
            main_here, tail_here, main_home, tail_home = homes[which]

            def gone(slot, carry):
                source = source_of(slot)

                @pl.when(source != me)
                def _():
                    pltpu.make_async_copy(
                        main_here.at[main_rows(slot)], main_home.at[main_rows(0)],
                        back_m.at[which, slot],
                    ).wait()
                    pltpu.make_async_copy(
                        tail_here.at[slot], tail_home.at[0], back_t.at[which, slot]
                    ).wait()

                return carry

            lax.fori_loop(0, slots, gone, 0)


def run_relay(*operands):
    bf16 = jnp.bfloat16
    vmem = pl.BlockSpec(memory_space=pltpu.VMEM)
    anywhere = pl.BlockSpec(memory_space=pl.ANY)
    dma = pltpu.SemaphoreType.DMA
    tokens = pltpu.VMEM((TOK, D), bf16)
    packed_main = pltpu.VMEM((EXPERTS * MAIN, D), bf16)
    packed_tail = pltpu.VMEM((EXPERTS, TAIL, D), bf16)
    home_main = pltpu.VMEM((PACKED, D), bf16)
    rows_in = pltpu.VMEM((ROWS, D), bf16)
    tails_in = pltpu.VMEM((SLOTS, TAIL, D), bf16)
    weight = pltpu.VMEM((WIDE, D), bf16)
    main_out = pltpu.VMEM((FIRST_TAIL, D), bf16)
    hidden = pltpu.VMEM((ROWS, WIDE), bf16)
    out = jax.ShapeDtypeStruct((TOK, D), bf16)
    return pl.pallas_call(
        relay_kernel,
        out_shape=(out, out),
        in_specs=[anywhere, vmem, anywhere, vmem, anywhere, anywhere, anywhere, vmem, vmem, vmem, vmem],
        out_specs=(vmem, vmem),
        scratch_shapes=[
            tokens, tokens, packed_main, packed_tail, packed_main, packed_tail, packed_main, packed_tail,
            home_main, packed_tail, home_main, packed_tail, pltpu.VMEM((TOK, D), jnp.float32),
            rows_in, tails_in, rows_in, tails_in, rows_in, tails_in,
            weight, weight, weight,
            main_out, tails_in, main_out, tails_in,
            hidden, hidden,
            pltpu.VMEM((ROWS - FIRST_TAIL, D), jnp.float32),
            pltpu.VMEM((EXPERTS * TAIL, D), jnp.float32),
            dma((2,)), dma((2,)), dma((3,)), dma((2, 3)), dma((SPLIT, 3)),
            dma((3, EXPERTS)), dma((3, EXPERTS)), dma((3, SLOTS)), dma((3, SLOTS)),
            dma((2, SLOTS)), dma((2, SLOTS)), dma((2, EXPERTS)), dma((2, EXPERTS)),
        ],
        compiler_params=pltpu.CompilerParams(
            collective_id=0, has_side_effects=True, vmem_limit_bytes=52 * 1024 * 1024
        ),
        name="relay",
    )(*operands)


def per_device(
    act_in,
    saved_in,
    grad_in,
    norm_gain,
    w_gate,
    w_up,
    w_down,
    routes_fwd,
    gates_fwd,
    routes_bwd,
    gates_bwd,
):
    act_out, grad_out = run_relay(
        act_in[0],
        saved_in[0],
        grad_in[0],
        norm_gain,
        w_gate[0].T,
        w_up[0].T,
        w_down[0],
        routes_fwd.reshape(1, TOK),
        gates_fwd.reshape(1, TOK),
        routes_bwd.reshape(1, TOK),
        gates_bwd.reshape(1, TOK),
    )
    return (act_out[None], grad_out[None])


def solution(mesh):
    in_specs = (
        P("section", "expert", None),
        P("section", "expert", None),
        P("section", "expert", None),
        P("section", None),
        P("section", None, "expert"),
        P("section", None, "expert"),
        P("section", "expert", None),
        P("section", "expert", None),
        P("section", "expert", None),
        P("section", "expert", None),
        P("section", "expert", None),
    )
    out_specs = (P("section", "expert", None), P("section", "expert", None))
    return jax.shard_map(
        per_device, mesh=mesh, in_specs=in_specs, out_specs=out_specs, check_vma=False
    )
```

time: 262 us -> 221 us (0.84)
  Pallas kernels: 232 us -> 216 us
  starting transfers between devices: 6.53 us -> 0 us
  waiting for transfers between devices: 5.72 us -> 0 us
  other arithmetic: 5.44 us -> 0 us
  matrix products: 5.04 us -> 0 us
    pallas_call x1, Pallas kernels: 232 us -> 216 us  [run_relay(): pl.pallas_call(relay_kernel, out_shape=(out, out), in_specs=[anywhere, vm...]
    ppermute x2 -> x0, starting transfers between devices: 6.53 us -> none  [passed_along(): return lax.ppermute(value, axis, pairs)]
    ppermute x2 -> x0, waiting for transfers between devices: 5.72 us -> none  [passed_along(): return lax.ppermute(value, axis, pairs)]
    dot_general x5 -> x0, matrix products: 5.04 us -> none  [the longest x2 2.9 us: brought_home(): lax.dot_general(chooser, rows, (((0,), (0,)), ((), ())), preferred_elemen...]
  transfers between devices with their start and end apart: 2 -> 0, of which waited for: 2 -> 0; matrix products, arithmetic and copies ran while one was open for 2% -> 0% of each run, Pallas kernels for 0% -> 0%
where the time goes in v2:
time: 221 us; the launch traced here: 220 us
  Pallas kernels  216 us (98%)
  local copies, waits for them, and re-layouts  3.31 us (1%)
    pallas_call x1, Pallas kernels, run_relay(): pl.pallas_call(relay_kernel, out_shape=(out, out), in_specs=[anywhere, vm...  216 us

profile of v2, /device:TPU:7, one launch (start us, length us, event | category | flops | bytes accessed | tf_op | source)
XLA Modules:
  0.0 220.2 jit_solution(11864148260458021453)
XLA Ops:
  0.6 0.0 copy-start.1
  0.6 0.0 copy-start.5
  0.7 0.0 copy-start.2
  0.7 0.0 copy-start.3
  0.7 0.0 copy-start.4
  0.7 0.6 copy-done.1
  1.3 0.0 copy-done.5
  1.3 0.0 copy-done.2
  1.3 0.0 copy-done.3
  1.3 0.0 copy-done.4
  1.4 0.0 copy-start
  1.4 1.0 copy-done
  2.4 216.2 %relay.1 = (bf16[128,2048]{1,0:T(8,128)(2,1)S(1)}, bf16[128,2048]{1,0:T(8,128)(2,1)S(1)}) custom-call(bf16[128,2048]{1,0:T(8,128)(2,1)S(1)} %bitcast.16, bf16[128,2048]{1,0:T(8,128)(2,1)} %bitcast.26, bf16[128,2048]{1,0:T(8,128)(2,1)} %bitcast.27, f32[1,2048]{1,0:T(1,128)S(1)} %copy-done.1, bf16[192,2048]{1,0:T(8,128)(2,1)} %bitcast.23, ...), custom_call_target="tpu_custom_call" | custom-call | tf_op jit(solution)/shard_map/relay/pallas_call | solution.py:560
  218.6 0.8 copy.15
  219.4 0.8 copy.16
Async XLA Ops:
  0.6 0.7 copy-start.1
  0.6 0.7 copy-start.5
  0.7 0.7 copy-start.2
  0.7 0.7 copy-start.3
  0.7 0.7 copy-start.4
  1.4 1.0 copy-start

commit v3 on v2

--- a/solution.py
+++ b/solution.py
@@ -12,15 +12,15 @@
 D = 2048
 TOK = 128
 UNITS = 192
+PIECES = 3
+PIECE = UNITS // PIECES
 WIDE = UNITS * SPLIT
 MAIN = 16
 TAIL = 2
 PACKED = EXPERTS * (MAIN + TAIL)
-EDGE_SLOTS = 14
-SLOTS = 18
+SLOTS = 16
 FIRST_TAIL = SLOTS * MAIN
-TAIL_ROWS = SLOTS * TAIL
-ROWS = 336
+ROWS = SLOTS * (MAIN + TAIL)
 RING = 16
 BLOCKS = RING // SPLIT
 TILE = 256
@@ -32,37 +32,32 @@
 
 def way(block, place, there):
     apart = lax.rem(there - block + BLOCKS, BLOCKS)
-    low = place < 2
+    first = place == 0
     to_edge = jnp.logical_or(
         apart == 1,
         jnp.logical_or(
-            jnp.logical_and(apart == 2, place >= 2), jnp.logical_and(apart == 0, place == 0)
+            jnp.logical_and(apart == 2, place >= 1), jnp.logical_and(apart == 0, first)
         ),
     )
     kind = jnp.where(
         apart == 0,
-        jnp.where(place == 0, 6, 5 + place),
-        jnp.where(apart == 2, jnp.where(low, 4 + place, 2 + place), place),
-    )
-    return jnp.where(to_edge, 0, 2), kind
+        jnp.where(first, 7, 4 + place),
+        jnp.where(apart == 2, jnp.where(first, 4, 3 + place), place),
+    )
+    return jnp.where(to_edge, 0, 1), kind
 
 
 def origin(block, place, slot):
     edge = place == 0
-    stride = jnp.where(edge, EDGE_SLOTS // 2, SLOTS // 2)
-    source_x = jnp.where(slot >= stride, 1, 0)
-    kind = slot - source_x * stride
-    apart = jnp.where(kind < 4, jnp.where(edge, 3, 1), jnp.where(kind < 6, 2, 0))
+    kind = lax.rem(slot, 8)
+    opposite = jnp.where(edge, 6, 4)
+    apart = jnp.where(kind < 4, jnp.where(edge, 3, 1), jnp.where(kind <= opposite, 2, 0))
     source_place = jnp.where(
         kind < 4,
         kind,
-        jnp.where(
-            kind < 6,
-            jnp.where(edge, kind - 2, kind - 4),
-            jnp.where(edge, 0, kind - 5),
-        ),
-    )
-    return source_x, lax.rem(block + apart, BLOCKS), source_place
+        jnp.where(edge, jnp.where(kind == 7, 0, kind - 3), kind - 4),
+    )
+    return slot // 8, lax.rem(block + apart, BLOCKS), source_place
 
 
 def relay_kernel(
@@ -86,9 +81,8 @@
     block = turned // SPLIT
     place = lax.rem(turned, SPLIT)
     edge = place == 0
-    middle = place == 2
-    computing = jnp.logical_or(edge, middle)
-    slots = jnp.where(edge, EDGE_SLOTS, SLOTS)
+    middle = place == 1
+    computing = place < 2
 
     def device(x, its_block, its_place):
         along = its_block * SPLIT + its_place
@@ -106,7 +100,7 @@
         x = number // BLOCKS
         there = lax.rem(number, BLOCKS)
         member, kind = way(block, place, there)
-        slot = x_lo * jnp.where(member == 0, EDGE_SLOTS // 2, SLOTS // 2) + kind
+        slot = x_lo * (SLOTS // 2) + kind
         return device(x, there, member), slot, expert_row(x, there)
 
     def source_of(slot):
@@ -142,16 +136,68 @@
 
             return carry
 
-        lax.fori_loop(0, slots, greet_source, 0)
-
-    @pl.when(edge)
-    def _():
-        signal("expert", neighbour(1))
-        signal("expert", neighbour(2))
-
-    @pl.when(jnp.logical_or(place == 1, middle))
-    def _():
-        signal("expert", neighbour(0))
+        lax.fori_loop(0, SLOTS, greet_source, 0)
+        signal("expert", neighbour(1 - place))
+
+    pl.semaphore_wait(barrier, jnp.where(computing, 7 + 15 + 1 + 2, 8 + 2))
+
+    weights = ((wg_in, wg), (wu_in, wu), (wd_in, wd))
+
+    def share_rows(share):
+        return pl.ds(pl.multiple_of(share * UNITS, UNITS), UNITS)
+
+    def piece_rows(start):
+        return pl.ds(pl.multiple_of(start, PIECE), PIECE)
+
+    def weight_copy(kind, piece, share, sent, dest, passed=False):
+        there = weights[kind][1].at[piece_rows(share * UNITS + piece * PIECE)]
+        return pltpu.make_async_remote_copy(
+            src_ref=there if passed else weights[kind][0].at[piece_rows(piece * PIECE)],
+            dst_ref=there,
+            send_sem=w_send.at[sent, kind, piece],
+            recv_sem=w_recv.at[share, kind, piece],
+            device_id={"expert": dest},
+            device_id_type=MESH,
+        )
+
+    def each_piece(body):
+        for kind in range(3):
+
+            def step(piece, carry):
+                body(kind, piece)
+                return carry
+
+            lax.fori_loop(0, PIECES, step, 0)
+
+    def hop(source, target, number, there):
+        return pltpu.make_async_remote_copy(
+            src_ref=source,
+            dst_ref=target,
+            send_sem=hop_send.at[number],
+            recv_sem=hop_recv.at[number],
+            device_id={"section": there},
+            device_id_type=MESH,
+        )
+
+    each_piece(
+        lambda kind, piece: weight_copy(
+            kind, piece, place, 0, neighbour(jnp.where(middle, 0, 1))
+        ).start()
+    )
+
+    for kind in range(3):
+        own = weights[kind][0]
+
+        @pl.when(computing)
+        def _():
+            pltpu.make_async_copy(
+                own, weights[kind][1].at[share_rows(place)], w_local.at[kind]
+            ).start()
+
+    hop_act = hop(act_in, x_new, 0, after)
+    hop_grad = hop(grad_in, dy, 1, ahead)
+    hop_act.start()
+    hop_grad.start()
 
     def one_hots(routes):
         down = lax.broadcasted_iota(jnp.int32, (TOK, TOK), 0)
@@ -201,71 +247,6 @@
         for expert in range(EXPERTS):
             tail[expert] = own_tails[expert * TAIL : (expert + 1) * TAIL, :].astype(jnp.bfloat16)
 
-    chooser_b, chosen_b = one_hots(routes_b)
-    inv_b = inverse_scale(saved_in)
-    pack(chooser_b, saved_in, inv_b, b_main, b_tail)
-
-    pl.semaphore_wait(
-        barrier,
-        jnp.where(edge, 24, jnp.where(middle, 27, jnp.where(place == 1, 11, 10))),
-    )
-
-    weights = ((wg_in, wg), (wu_in, wu), (wd_in, wd))
-
-    def share_rows(share):
-        return pl.ds(pl.multiple_of(share * UNITS, UNITS), UNITS)
-
-    def weight_copy(kind, source, share, sent, dest):
-        return pltpu.make_async_remote_copy(
-            src_ref=source,
-            dst_ref=weights[kind][1].at[share_rows(share)],
-            send_sem=w_send.at[sent, kind],
-            recv_sem=w_recv.at[share, kind],
-            device_id={"expert": dest},
-            device_id_type=MESH,
-        )
-
-    def hop(source, target, number, there):
-        return pltpu.make_async_remote_copy(
-            src_ref=source,
-            dst_ref=target,
-            send_sem=hop_send.at[number],
-            recv_sem=hop_recv.at[number],
-            device_id={"section": there},
-            device_id_type=MESH,
-        )
-
-    hop_act = hop(act_in, x_new, 0, after)
-    hop_grad = hop(grad_in, dy, 1, ahead)
-    hop_act.start()
-    hop_grad.start()
-
-    for kind in range(3):
-        own = weights[kind][0]
-
-        @pl.when(edge)
-        def _():
-            weight_copy(kind, own, 0, 0, neighbour(2)).start()
-
-        @pl.when(place == 1)
-        def _():
-            weight_copy(kind, own, 1, 0, neighbour(0)).start()
-            weight_copy(kind, own, 1, 1, neighbour(2)).start()
-
-        @pl.when(middle)
-        def _():
-            weight_copy(kind, own, 2, 0, neighbour(0)).start()
-
-        @pl.when(place == 3)
-        def _():
-            weight_copy(kind, own, 3, 0, neighbour(2)).start()
-
-        @pl.when(computing)
-        def _():
-            pltpu.make_async_copy(
-                own, weights[kind][1].at[share_rows(place)], w_local.at[kind]
-            ).start()
-
     streams = (
         (f_main, f_tail, xf, xft),
         (b_main, b_tail, xb, xbt),
@@ -305,17 +286,18 @@
 
         lax.fori_loop(0, EXPERTS, body, 0)
 
+    chooser_b, chosen_b = one_hots(routes_b)
+    inv_b = inverse_scale(saved_in)
+    pack(chooser_b, saved_in, inv_b, b_main, b_tail)
     send_stream(1)
+
+    hop_grad.wait_recv()
+    pack(chooser_b, dy, None, g_main, g_tail)
+    send_stream(2)
 
     chooser_f, chosen_f = one_hots(routes_f)
     hop_act.wait_recv()
     pack(chooser_f, x_new, inverse_scale(x_new), f_main, f_tail)
-    send_stream(0)
-
-    hop_grad.wait_recv()
-    pack(chooser_b, dy, None, g_main, g_tail)
-    send_stream(2)
-
     def wait_stream(stream):
         main_in, tail_in, main_there, tail_there = streams[stream]
 
@@ -328,7 +310,7 @@
             ).wait()
             return carry
 
-        lax.fori_loop(0, slots, body, 0)
+        lax.fori_loop(0, SLOTS, body, 0)
         for slot in range(SLOTS):
             tail_rows[slot * TAIL : (slot + 1) * TAIL, :] = tail_there[slot].astype(jnp.float32)
         main_there[FIRST_TAIL:ROWS, :] = tail_rows[...].astype(jnp.bfloat16)
@@ -359,7 +341,7 @@
 
             return carry
 
-        lax.fori_loop(0, slots, body, 0)
+        lax.fori_loop(0, SLOTS, body, 0)
 
     def cols(step):
         return pl.ds(pl.multiple_of(step * TILE, TILE), TILE)
@@ -380,10 +362,12 @@
 
     @pl.when(middle)
     def _():
-        for kind in range(3):
-            held = weights[kind][1].at[share_rows(3)]
-            weight_copy(kind, held, 3, 0, neighbour(0)).wait_recv()
-            weight_copy(kind, held, 3, 1, neighbour(0)).start()
+        def pass_on(kind, piece):
+            for share in (2, 3):
+                weight_copy(kind, piece, share, 0, neighbour(0)).wait_recv()
+                weight_copy(kind, piece, share, share - 1, neighbour(0), True).start()
+
+        each_piece(pass_on)
 
     @pl.when(computing)
     def _():
@@ -391,35 +375,27 @@
             own = weights[kind][0]
             held = weights[kind][1].at[share_rows(place)]
             pltpu.make_async_copy(own, held, w_local.at[kind]).wait()
-            weight_copy(kind, held, 1, 0, neighbour(0)).wait_recv()
-            weight_copy(kind, held, jnp.where(edge, 2, 0), 0, neighbour(0)).wait_recv()
+
+        each_piece(
+            lambda kind, piece: weight_copy(kind, piece, 1 - place, 0, neighbour(0)).wait_recv()
+        )
 
         @pl.when(edge)
         def _():
-            for kind in range(3):
-                held = weights[kind][1].at[share_rows(3)]
-                weight_copy(kind, held, 3, 0, neighbour(0)).wait_recv()
-
-        wait_stream(0)
-
-        def forward_hidden(step, carry):
-            gate_pre = dot_nt(xf[...], wg[cols(step), :])
-            up_pre = dot_nt(xf[...], wu[cols(step), :])
-            hid_a[:, cols(step)] = (gate_pre * jax.nn.sigmoid(gate_pre) * up_pre).astype(
-                jnp.bfloat16
-            )
-            return carry
-
-        lax.fori_loop(0, WIDE // TILE, forward_hidden, 0)
-
-        def forward_out(step, carry):
-            put_result(yf, step, dot_nn(hid_a[...], wd[:, cols(step)]))
-            return carry
-
-        lax.fori_loop(0, D // TILE, forward_out, 0)
-        put_tails(yft)
-        send_back(0, yf, yft, home_f, home_ft)
-
+            def arrived(kind, piece):
+                for share in (2, 3):
+                    weight_copy(kind, piece, share, 0, neighbour(0)).wait_recv()
+
+            each_piece(arrived)
+
+    @pl.when(jnp.logical_not(computing))
+    def _():
+        each_piece(lambda kind, piece: weight_copy(kind, piece, 0, 0, neighbour(0)).wait_send())
+
+    send_stream(0)
+
+    @pl.when(computing)
+    def _():
         wait_stream(1)
         wait_stream(2)
 
@@ -445,6 +421,26 @@
         put_tails(ybt)
         send_back(1, yb, ybt, home_b, home_bt)
 
+        wait_stream(0)
+
+        def forward_hidden(step, carry):
+            gate_pre = dot_nt(xf[...], wg[cols(step), :])
+            up_pre = dot_nt(xf[...], wu[cols(step), :])
+            hid_a[:, cols(step)] = (gate_pre * jax.nn.sigmoid(gate_pre) * up_pre).astype(
+                jnp.bfloat16
+            )
+            return carry
+
+        lax.fori_loop(0, WIDE // TILE, forward_hidden, 0)
+
+        def forward_out(step, carry):
+            put_result(yf, step, dot_nn(hid_a[...], wd[:, cols(step)]))
+            return carry
+
+        lax.fori_loop(0, D // TILE, forward_out, 0)
+        put_tails(yft)
+        send_back(0, yf, yft, home_f, home_ft)
+
     homes = ((yf, yft, home_f, home_ft), (yb, ybt, home_b, home_bt))
 
     def wait_home(which):
@@ -463,13 +459,6 @@
         for expert in range(EXPERTS):
             own_tails[expert * TAIL : (expert + 1) * TAIL, :] = tail_home[expert].astype(jnp.float32)
         main_home[EXPERTS * MAIN :, :] = own_tails[...].astype(jnp.bfloat16)
-
-    wait_home(0)
-    gate_f = as_column(gates_f)
-    for step in range(D // TILE):
-        part = static_cols(step)
-        mixed = dot_nn(chosen_f, home_f[:, part]) * gate_f
-        act_out[:, part] = (x_new[:, part].astype(jnp.float32) + mixed).astype(jnp.bfloat16)
 
     wait_home(1)
     gate_b = as_column(gates_b)
@@ -488,6 +477,13 @@
         d_input = inv_scale * (scaled[:, part] - saved_in[:, part].astype(jnp.float32) * fold)
         grad_out[:, part] = (dy[:, part].astype(jnp.float32) + d_input).astype(jnp.bfloat16)
 
+    wait_home(0)
+    gate_f = as_column(gates_f)
+    for step in range(D // TILE):
+        part = static_cols(step)
+        mixed = dot_nn(chosen_f, home_f[:, part]) * gate_f
+        act_out[:, part] = (x_new[:, part].astype(jnp.float32) + mixed).astype(jnp.bfloat16)
+
     hop_act.wait_send()
     hop_grad.wait_send()
 
@@ -511,13 +507,17 @@
 
         lax.fori_loop(0, EXPERTS, left, 0)
 
-    for kind in range(3):
-        weight_copy(kind, weights[kind][0], 0, 0, neighbour(0)).wait_send()
-
-    @pl.when(jnp.logical_or(place == 1, middle))
-    def _():
-        for kind in range(3):
-            weight_copy(kind, weights[kind][0], 0, 1, neighbour(0)).wait_send()
+    @pl.when(computing)
+    def _():
+        each_piece(lambda kind, piece: weight_copy(kind, piece, 0, 0, neighbour(0)).wait_send())
+
+    @pl.when(middle)
+    def _():
+        def passed_on(kind, piece):
+            for sent in (1, 2):
+                weight_copy(kind, piece, 0, sent, neighbour(0)).wait_send()
+
+        each_piece(passed_on)
 
     @pl.when(computing)
     def _():
@@ -539,7 +539,7 @@
 
                 return carry
 
-            lax.fori_loop(0, slots, gone, 0)
+            lax.fori_loop(0, SLOTS, gone, 0)
 
 
 def run_relay(*operands):
@@ -571,7 +571,7 @@
             hidden, hidden,
             pltpu.VMEM((ROWS - FIRST_TAIL, D), jnp.float32),
             pltpu.VMEM((EXPERTS * TAIL, D), jnp.float32),
-            dma((2,)), dma((2,)), dma((3,)), dma((2, 3)), dma((SPLIT, 3)),
+            dma((2,)), dma((2,)), dma((3,)), dma((3, 3, PIECES)), dma((SPLIT, 3, PIECES)),
             dma((3, EXPERTS)), dma((3, EXPERTS)), dma((3, SLOTS)), dma((3, SLOTS)),
             dma((2, SLOTS)), dma((2, SLOTS)), dma((2, EXPERTS)), dma((2, EXPERTS)),
         ],

time: 221 us -> 216 us (0.977)
  Pallas kernels: 216 us -> 212 us
    pallas_call x1, Pallas kernels: 216 us -> 212 us  [run_relay(): pl.pallas_call(relay_kernel, out_shape=(out, out), in_specs=[anywhere, vm...]
where the time goes in v3:
time: 216 us
  Pallas kernels  212 us (98%)
  local copies, waits for them, and re-layouts  3.31 us (2%)
    pallas_call x1, Pallas kernels, run_relay(): pl.pallas_call(relay_kernel, out_shape=(out, out), in_specs=[anywhere, vm...  212 us

profile of v3, /device:TPU:7, one launch (start us, length us, event | category | flops | bytes accessed | tf_op | source)
XLA Modules:
  0.0 215.8 jit_solution(3494559998450455592)
XLA Ops:
  0.6 0.0 copy-start.1
  0.6 0.0 copy-start.5
  0.7 0.0 copy-start.2
  0.7 0.0 copy-start.3
  0.7 0.0 copy-start.4
  0.7 0.6 copy-done.1
  1.3 0.0 copy-done.5
  1.3 0.0 copy-done.2
  1.3 0.0 copy-done.3
  1.3 0.0 copy-done.4
  1.4 0.0 copy-start
  1.4 1.0 copy-done
  2.4 211.8 %relay.1 = (bf16[128,2048]{1,0:T(8,128)(2,1)S(1)}, bf16[128,2048]{1,0:T(8,128)(2,1)S(1)}) custom-call(bf16[128,2048]{1,0:T(8,128)(2,1)S(1)} %bitcast.16, bf16[128,2048]{1,0:T(8,128)(2,1)} %bitcast.26, bf16[128,2048]{1,0:T(8,128)(2,1)} %bitcast.27, f32[1,2048]{1,0:T(1,128)S(1)} %copy-done.1, bf16[192,2048]{1,0:T(8,128)(2,1)} %bitcast.23, ...), custom_call_target="tpu_custom_call" | custom-call | tf_op jit(solution)/shard_map/relay/pallas_call | solution.py:560
  214.2 0.8 copy.15
  215.0 0.8 copy.16
Async XLA Ops:
  0.6 0.7 copy-start.1
  0.6 0.7 copy-start.5
  0.7 0.7 copy-start.2
  0.7 0.7 copy-start.3
  0.7 0.7 copy-start.4
  1.4 1.0 copy-start

commit v4 on v3

--- a/solution.py
+++ b/solution.py
@@ -293,7 +293,9 @@
 
     hop_grad.wait_recv()
     pack(chooser_b, dy, None, g_main, g_tail)
-    send_stream(2)
+    @pl.when(jnp.logical_not(middle))
+    def _():
+        send_stream(2)
 
     chooser_f, chosen_f = one_hots(routes_f)
     hop_act.wait_recv()
@@ -368,6 +370,7 @@
                 weight_copy(kind, piece, share, share - 1, neighbour(0), True).start()
 
         each_piece(pass_on)
+        send_stream(2)
 
     @pl.when(computing)
     def _():
@@ -460,8 +463,9 @@
             own_tails[expert * TAIL : (expert + 1) * TAIL, :] = tail_home[expert].astype(jnp.float32)
         main_home[EXPERTS * MAIN :, :] = own_tails[...].astype(jnp.bfloat16)
 
+    gate_f = as_column(gates_f)
+    gate_b = as_column(gates_b)
     wait_home(1)
-    gate_b = as_column(gates_b)
     total = jnp.zeros((TOK, 1), jnp.float32)
     for step in range(D // TILE):
         part = static_cols(step)
@@ -478,7 +482,6 @@
         grad_out[:, part] = (dy[:, part].astype(jnp.float32) + d_input).astype(jnp.bfloat16)
 
     wait_home(0)
-    gate_f = as_column(gates_f)
     for step in range(D // TILE):
         part = static_cols(step)
         mixed = dot_nn(chosen_f, home_f[:, part]) * gate_f
@@ -545,7 +548,7 @@
 def run_relay(*operands):
     bf16 = jnp.bfloat16
     vmem = pl.BlockSpec(memory_space=pltpu.VMEM)
-    anywhere = pl.BlockSpec(memory_space=pl.ANY)
+    anywhere = pl.BlockSpec(memory_space=pltpu.HBM)
     dma = pltpu.SemaphoreType.DMA
     tokens = pltpu.VMEM((TOK, D), bf16)
     packed_main = pltpu.VMEM((EXPERTS * MAIN, D), bf16)

time: 216 us -> 214 us (level)
  no operation moved by 1% of the time
where the time goes in v4:
time: 214 us
  Pallas kernels  210 us (98%)
  local copies, waits for them, and re-layouts  3.31 us (2%)
    pallas_call x1, Pallas kernels, run_relay(): pl.pallas_call(relay_kernel, out_shape=(out, out), in_specs=[anywhere, vm...  210 us

profile of v4, /device:TPU:7, one launch (start us, length us, event | category | flops | bytes accessed | tf_op | source)
XLA Modules:
  0.0 213.7 jit_solution(3721953494173619382)
XLA Ops:
  0.6 0.0 copy-start.1
  0.6 0.0 copy-start.5
  0.7 0.0 copy-start.2
  0.7 0.0 copy-start.3
  0.7 0.0 copy-start.4
  0.7 0.6 copy-done.1
  1.3 0.0 copy-done.5
  1.3 0.0 copy-done.2
  1.3 0.0 copy-done.3
  1.3 0.0 copy-done.4
  1.4 0.0 copy-start
  1.4 1.0 copy-done
  2.4 209.7 %relay.1 = (bf16[128,2048]{1,0:T(8,128)(2,1)S(1)}, bf16[128,2048]{1,0:T(8,128)(2,1)S(1)}) custom-call(bf16[128,2048]{1,0:T(8,128)(2,1)S(1)} %bitcast.16, bf16[128,2048]{1,0:T(8,128)(2,1)} %bitcast.26, bf16[128,2048]{1,0:T(8,128)(2,1)} %bitcast.27, f32[1,2048]{1,0:T(1,128)S(1)} %copy-done.1, bf16[192,2048]{1,0:T(8,128)(2,1)} %bitcast.23, ...), custom_call_target="tpu_custom_call" | custom-call | tf_op jit(solution)/shard_map/relay/pallas_call | solution.py:563
  212.1 0.8 copy.15
  212.9 0.8 copy.16
Async XLA Ops:
  0.6 0.7 copy-start.1
  0.6 0.7 copy-start.5
  0.7 0.7 copy-start.2
  0.7 0.7 copy-start.3
  0.7 0.7 copy-start.4
  1.4 1.0 copy-start

commit v5 on v4

--- a/solution.py
+++ b/solution.py
@@ -12,7 +12,7 @@
 D = 2048
 TOK = 128
 UNITS = 192
-PIECES = 3
+PIECES = 2
 PIECE = UNITS // PIECES
 WIDE = UNITS * SPLIT
 MAIN = 16

time: 214 us -> 214 us (level)
  no operation moved by 1% of the time
where the time goes in v5:
time: 214 us
  Pallas kernels  210 us (98%)
  local copies, waits for them, and re-layouts  3.31 us (2%)
    pallas_call x1, Pallas kernels, run_relay(): pl.pallas_call(relay_kernel, out_shape=(out, out), in_specs=[anywhere, vm...  210 us

profile of v5, /device:TPU:7, one launch (start us, length us, event | category | flops | bytes accessed | tf_op | source)
XLA Modules:
  0.0 213.5 jit_solution(10087579362532815073)
XLA Ops:
  0.6 0.0 copy-start.1
  0.6 0.0 copy-start.5
  0.7 0.0 copy-start.2
  0.7 0.0 copy-start.3
  0.7 0.0 copy-start.4
  0.7 0.6 copy-done.1
  1.3 0.0 copy-done.5
  1.3 0.0 copy-done.2
  1.3 0.0 copy-done.3
  1.3 0.0 copy-done.4
  1.4 0.0 copy-start
  1.4 1.0 copy-done
  2.4 209.5 %relay.1 = (bf16[128,2048]{1,0:T(8,128)(2,1)S(1)}, bf16[128,2048]{1,0:T(8,128)(2,1)S(1)}) custom-call(bf16[128,2048]{1,0:T(8,128)(2,1)S(1)} %bitcast.16, bf16[128,2048]{1,0:T(8,128)(2,1)} %bitcast.26, bf16[128,2048]{1,0:T(8,128)(2,1)} %bitcast.27, f32[1,2048]{1,0:T(1,128)S(1)} %copy-done.1, bf16[192,2048]{1,0:T(8,128)(2,1)} %bitcast.23, ...), custom_call_target="tpu_custom_call" | custom-call | tf_op jit(solution)/shard_map/relay/pallas_call | solution.py:563
  211.9 0.8 copy.15
  212.7 0.8 copy.16
Async XLA Ops:
  0.6 0.7 copy-start.1
  0.6 0.7 copy-start.5
  0.7 0.7 copy-start.2
  0.7 0.7 copy-start.3
  0.7 0.7 copy-start.4
  1.4 1.0 copy-start
